TPU v7x, 32 devices: a whole 2x2x4 slice. The times are simulated.
32 devices in a mesh: dp: 16 (over z, y, core), fsdp: 2 (over x).
Axes of the slice: x: 2, y: 2, z: 4, core: 2. Of those that a mesh axis runs over, the one named last changes fastest.
Arguments:
- tokens: bfloat16 [64, 280, 768], P(('dp', 'fsdp')), may hold values from -6 to 6
- patch_counts: int32 [64], P(('dp', 'fsdp')), may hold values from 100 to 240, as said below
- cotangent: bfloat16 [64, 280, 768], P(('dp', 'fsdp')), may hold values from -6 to 6
- norm1_gain: bfloat16 [768], P('fsdp'), may hold values from 0.5 to 1.5
- norm1_bias: bfloat16 [768], P('fsdp'), may hold values from -1.796875 to 1.796875
- qkv_weight: bfloat16 [768, 2304], P('fsdp'), may hold values from -0.21875 to 0.21875
- qv_bias: bfloat16 [1536], P('fsdp'), may hold values from -1.796875 to 1.796875
- out_weight: bfloat16 [768, 768], P('fsdp'), may hold values from -0.875 to 0.875
- out_bias: bfloat16 [768], P('fsdp'), may hold values from -1.796875 to 1.796875
- norm2_gain: bfloat16 [768], P('fsdp'), may hold values from 0.5 to 1.5
- norm2_bias: bfloat16 [768], P('fsdp'), may hold values from -1.796875 to 1.796875
- up_weight: bfloat16 [768, 3072], P('fsdp'), may hold values from -0.21875 to 0.21875
- up_bias: bfloat16 [3072], P('fsdp'), may hold values from -1.796875 to 1.796875
- down_weight: bfloat16 [3072, 768], P('fsdp'), may hold values from -0.109375 to 0.109375
- down_bias: bfloat16 [768], P('fsdp'), may hold values from -1.796875 to 1.796875
Outputs:
- result: bfloat16 [64, 280, 768], P(('dp', 'fsdp'))
- grad_tokens: bfloat16 [64, 280, 768], P(('dp', 'fsdp'))
- grad_norm1_gain: float32 [768], P('fsdp')
- grad_norm1_bias: float32 [768], P('fsdp')
- grad_qkv_weight: float32 [768, 2304], P('fsdp')
- grad_qv_bias: float32 [1536], P('fsdp')
- grad_out_weight: float32 [768, 768], P('fsdp')
- grad_out_bias: float32 [768], P('fsdp')
- grad_norm2_gain: float32 [768], P('fsdp')
- grad_norm2_bias: float32 [768], P('fsdp')
- grad_up_weight: float32 [768, 3072], P('fsdp')
- grad_up_bias: float32 [3072], P('fsdp')
- grad_down_weight: float32 [3072, 768], P('fsdp')
- grad_down_bias: float32 [768], P('fsdp')
Inputs may be any that keep to these rules, and one draw needn't show every extreme that they name: `patch_counts`: patches of each pair; some pair has exactly 240 and some exactly 100.
All inputs are finite; a program needn't handle non-finite values.
Results may differ from a plain program's by a relative error of at most 0.014.
Values may be sent and summed in bfloat16 or wider, within the bound.
A program may use at most 192 MiB of HBM per device.

v0:
```python
import jax
import jax.numpy as jnp
from jax import lax
from jax.sharding import PartitionSpec as P

HEAD_DIM = 64
TEXT = 40


norm_eps = 1e-06


def normalize(values, gain, shift):
    centered = values - jnp.mean(values, axis=-1, keepdims=True)
    variance = jnp.mean(centered * centered, axis=-1, keepdims=True)
    inverse = lax.rsqrt(variance + norm_eps)
    normed = centered * inverse
    return (normed * gain + shift, normed, inverse)


def norm_back(grad_scaled, normed, inverse):
    first = jnp.mean(grad_scaled, axis=-1, keepdims=True)
    second = jnp.mean(grad_scaled * normed, axis=-1, keepdims=True)
    return inverse * (grad_scaled - first - normed * second)


def gelu_exact(values):
    return jax.nn.gelu(values, approximate=False)


def on_device(
    tokens,
    patch_counts,
    cotangent,
    norm1_gain,
    norm1_bias,
    qkv_weight,
    qv_bias,
    out_weight,
    out_bias,
    norm2_gain,
    norm2_bias,
    up_weight,
    up_bias,
    down_weight,
    down_bias,
):
    f32 = jnp.float32
    bf16 = jnp.bfloat16
    pairs, length, width = tokens.shape
    rows = pairs * length
    heads = width // HEAD_DIM
    attn_full = (
        lax.all_gather(norm1_gain, "fsdp", axis=0, tiled=True),
        lax.all_gather(norm1_bias, "fsdp", axis=0, tiled=True),
        lax.all_gather(qkv_weight, "fsdp", axis=0, tiled=True),
        lax.all_gather(qv_bias, "fsdp", axis=0, tiled=True),
        lax.all_gather(out_weight, "fsdp", axis=0, tiled=True),
        lax.all_gather(out_bias, "fsdp", axis=0, tiled=True),
    )
    mlp_full = (
        lax.all_gather(norm2_gain, "fsdp", axis=0, tiled=True),
        lax.all_gather(norm2_bias, "fsdp", axis=0, tiled=True),
        lax.all_gather(up_weight, "fsdp", axis=0, tiled=True),
        lax.all_gather(up_bias, "fsdp", axis=0, tiled=True),
        lax.all_gather(down_weight, "fsdp", axis=0, tiled=True),
        lax.all_gather(down_bias, "fsdp", axis=0, tiled=True),
    )
    gain_one, shift_one, weight_qkv, bias_qv, weight_out, bias_out = attn_full
    gain_two, shift_two, weight_up, bias_up, weight_down, bias_down = mlp_full
    x_input = tokens.reshape(rows, width).astype(f32)
    normed_one, unit_one, inverse_one = normalize(
        x_input, gain_one.astype(f32), shift_one.astype(f32)
    )
    normed_one_b = normed_one.astype(bf16)
    bias_qv_f = bias_qv.astype(f32)
    bias_full = jnp.concatenate([bias_qv_f[:width], jnp.zeros((width,), f32), bias_qv_f[width:]])
    packed = (jnp.dot(normed_one_b, weight_qkv, preferred_element_type=f32) + bias_full).astype(
        bf16
    )
    packed = packed.reshape(pairs, length, 3, heads, HEAD_DIM)
    query = packed[:, :, 0]
    keys = packed[:, :, 1]
    values_all = packed[:, :, 2]
    valid = lax.broadcasted_iota(jnp.int32, (pairs, length), 1) < (TEXT + patch_counts)[:, None]
    valid = valid[:, None, None, :]

    def scores_of(query_rows, key_rows):
        raw = (
            jnp.einsum("plhd,pmhd->phlm", query_rows, key_rows, preferred_element_type=f32) * 0.125
        )
        return jnp.where(valid, raw, -1e30)

    scores = scores_of(query, keys)
    peak = jnp.max(scores, axis=-1, keepdims=True)
    log_total = peak + jnp.log(jnp.sum(jnp.exp(scores - peak), axis=-1, keepdims=True))
    probs_b = jnp.exp(scores - log_total).astype(bf16)
    attended = jnp.einsum("phlm,pmhd->plhd", probs_b, values_all, preferred_element_type=f32)
    attended = attended.astype(bf16).reshape(rows, width)
    middle = (
        x_input + jnp.dot(attended, weight_out, preferred_element_type=f32) + bias_out.astype(f32)
    )
    gain_two_f = gain_two.astype(f32)
    normed_two, unit_two, inverse_two = normalize(middle, gain_two_f, shift_two.astype(f32))
    normed_two_b = normed_two.astype(bf16)
    hidden = jnp.dot(normed_two_b, weight_up, preferred_element_type=f32) + bias_up.astype(f32)
    active, gelu_pull = jax.vjp(gelu_exact, hidden)
    active_b = active.astype(bf16)
    output = (
        middle + jnp.dot(active_b, weight_down, preferred_element_type=f32) + bias_down.astype(f32)
    )
    result = output.astype(bf16).reshape(pairs, length, width)
    again = (
        lax.all_gather(norm1_gain, "fsdp", axis=0, tiled=True),
        lax.all_gather(qkv_weight, "fsdp", axis=0, tiled=True),
        lax.all_gather(out_weight, "fsdp", axis=0, tiled=True),
        lax.all_gather(norm2_gain, "fsdp", axis=0, tiled=True),
        lax.all_gather(up_weight, "fsdp", axis=0, tiled=True),
        lax.all_gather(down_weight, "fsdp", axis=0, tiled=True),
    )
    gain_back_one, weight_qkv_back, weight_out_back, gain_two, weight_up_back, weight_down_back = (
        again
    )
    gain_two_f = gain_two.astype(f32)
    grad_out_b = cotangent.reshape(rows, width)
    grad_out_f = grad_out_b.astype(f32)
    grad_down = jnp.dot(active_b.T, grad_out_b, preferred_element_type=f32)
    grad_down_bias = jnp.sum(grad_out_f, axis=0)
    grad_active = jnp.dot(grad_out_b, weight_down_back.T, preferred_element_type=f32)
    grad_hidden_b = gelu_pull(grad_active)[0].astype(bf16)
    grad_up = jnp.dot(normed_two_b.T, grad_hidden_b, preferred_element_type=f32)
    grad_up_bias = jnp.sum(grad_hidden_b.astype(f32), axis=0)
    grad_normed_two = jnp.dot(grad_hidden_b, weight_up_back.T, preferred_element_type=f32)
    grad_gain_two = jnp.sum(grad_normed_two * unit_two, axis=0)
    grad_shift_two = jnp.sum(grad_normed_two, axis=0)
    grad_middle = grad_out_f + norm_back(grad_normed_two * gain_two_f, unit_two, inverse_two)
    grad_middle_b = grad_middle.astype(bf16)
    grad_weight_out = jnp.dot(attended.T, grad_middle_b, preferred_element_type=f32)
    grad_bias_out = jnp.sum(grad_middle_b.astype(f32), axis=0)
    grad_attended = jnp.dot(grad_middle_b, weight_out_back.T, preferred_element_type=f32)
    grad_attended = grad_attended.astype(bf16).reshape(pairs, length, heads, HEAD_DIM)
    probs_again = jnp.exp(scores_of(query, keys) - log_total)
    probs_again_b = probs_again.astype(bf16)
    grad_probs = jnp.einsum(
        "plhd,pmhd->phlm", grad_attended, values_all, preferred_element_type=f32
    )
    grad_values = jnp.einsum(
        "phlm,plhd->pmhd", probs_again_b, grad_attended, preferred_element_type=f32
    )
    row_dot = jnp.sum(probs_again * grad_probs, axis=-1, keepdims=True)
    grad_scores_b = (probs_again * (grad_probs - row_dot)).astype(bf16)
    grad_query = (
        jnp.einsum("phlm,pmhd->plhd", grad_scores_b, keys, preferred_element_type=f32) * 0.125
    )
    grad_keys = (
        jnp.einsum("phlm,plhd->pmhd", grad_scores_b, query, preferred_element_type=f32) * 0.125
    )
    grad_packed = (
        jnp.stack([grad_query, grad_keys, grad_values], axis=2)
        .astype(bf16)
        .reshape(rows, 3 * width)
    )
    grad_weight_qkv = jnp.dot(normed_one_b.T, grad_packed, preferred_element_type=f32)
    column_sums = jnp.sum(grad_packed.astype(f32), axis=0)
    grad_bias_qv = jnp.concatenate([column_sums[:width], column_sums[2 * width :]])
    grad_normed_one = jnp.dot(grad_packed, weight_qkv_back.T, preferred_element_type=f32)
    grad_gain_one = jnp.sum(grad_normed_one * unit_one, axis=0)
    grad_shift_one = jnp.sum(grad_normed_one, axis=0)
    grad_input = grad_middle + norm_back(
        grad_normed_one * gain_back_one.astype(f32), unit_one, inverse_one
    )
    gradients = (
        grad_gain_one,
        grad_shift_one,
        grad_weight_qkv,
        grad_bias_qv,
        grad_weight_out,
        grad_bias_out,
        grad_gain_two,
        grad_shift_two,
        grad_up,
        grad_up_bias,
        grad_down,
        grad_down_bias,
    )
    pieces = (
        lax.psum_scatter(
            gradients[0].astype(jnp.bfloat16), "fsdp", scatter_dimension=0, tiled=True
        ).astype(jnp.float32),
        lax.psum_scatter(
            gradients[1].astype(jnp.bfloat16), "fsdp", scatter_dimension=0, tiled=True
        ).astype(jnp.float32),
        lax.psum_scatter(
            gradients[2].astype(jnp.bfloat16), "fsdp", scatter_dimension=0, tiled=True
        ).astype(jnp.float32),
        lax.psum_scatter(
            gradients[3].astype(jnp.bfloat16), "fsdp", scatter_dimension=0, tiled=True
        ).astype(jnp.float32),
        lax.psum_scatter(
            gradients[4].astype(jnp.bfloat16), "fsdp", scatter_dimension=0, tiled=True
        ).astype(jnp.float32),
        lax.psum_scatter(
            gradients[5].astype(jnp.bfloat16), "fsdp", scatter_dimension=0, tiled=True
        ).astype(jnp.float32),
        lax.psum_scatter(
            gradients[6].astype(jnp.bfloat16), "fsdp", scatter_dimension=0, tiled=True
        ).astype(jnp.float32),
        lax.psum_scatter(
            gradients[7].astype(jnp.bfloat16), "fsdp", scatter_dimension=0, tiled=True
        ).astype(jnp.float32),
        lax.psum_scatter(
            gradients[8].astype(jnp.bfloat16), "fsdp", scatter_dimension=0, tiled=True
        ).astype(jnp.float32),
        lax.psum_scatter(
            gradients[9].astype(jnp.bfloat16), "fsdp", scatter_dimension=0, tiled=True
        ).astype(jnp.float32),
        lax.psum_scatter(
            gradients[10].astype(jnp.bfloat16), "fsdp", scatter_dimension=0, tiled=True
        ).astype(jnp.float32),
        lax.psum_scatter(
            gradients[11].astype(jnp.bfloat16), "fsdp", scatter_dimension=0, tiled=True
        ).astype(jnp.float32),
    )
    shares = lax.psum(
        (
            pieces[0],
            pieces[1],
            pieces[2],
            pieces[3],
            pieces[4],
            pieces[5],
            pieces[6],
            pieces[7],
            pieces[8],
            pieces[9],
            pieces[10],
            pieces[11],
        ),
        "dp",
    )
    return (
        result,
        grad_input.astype(bf16).reshape(pairs, length, width),
        shares[0],
        shares[1],
        shares[2],
        shares[3],
        shares[4],
        shares[5],
        shares[6],
        shares[7],
        shares[8],
        shares[9],
        shares[10],
        shares[11],
    )


def solution(mesh):
    return jax.shard_map(
        on_device,
        mesh=mesh,
        in_specs=(
            P(("dp", "fsdp"), None, None),
            P(("dp", "fsdp")),
            P(("dp", "fsdp"), None, None),
            P("fsdp"),
            P("fsdp"),
            P("fsdp", None),
            P("fsdp"),
            P("fsdp", None),
            P("fsdp"),
            P("fsdp"),
            P("fsdp"),
            P("fsdp", None),
            P("fsdp"),
            P("fsdp", None),
            P("fsdp"),
        ),
        out_specs=(
            P(("dp", "fsdp"), None, None),
            P(("dp", "fsdp"), None, None),
            P("fsdp"),
            P("fsdp"),
            P("fsdp", None),
            P("fsdp"),
            P("fsdp", None),
            P("fsdp"),
            P("fsdp"),
            P("fsdp"),
            P("fsdp", None),
            P("fsdp"),
            P("fsdp", None),
            P("fsdp"),
        ),
        check_vma=False,
    )
```

profile of v0, /device:TPU:0, one launch (start us, length us, event | category | flops | bytes accessed | tf_op | source)
XLA Modules:
  0.0 774.3 jit_solution(4300698028435527824)
XLA Ops:
  10.9 5.2 all-gather
  16.2 4.3 all-gather.1
  20.6 4.3 all-gather.3
  25.0 4.3 all-gather.4
  29.4 4.3 all-gather.5
  33.8 4.4 all-gather.2
  38.3 4.5 all-gather.6
  45.6 16.3 %all-gather.13.cloned.1.call-done = bf16[768,2304]{1,0:T(8,128)(2,1)} async-done(((bf16[384,2304]{1,0:T(8,128)(2,1)}), bf16[768,2304]{1,0:T(8,128)(2,1)}) %all-gather.13.cloned.1.call-update) | async-done | bytes 3538960 | tf_op jit(solution)/shard_map/all_gather | solution.py:56
  61.9 4.7 add_convert_fusion.1
  66.7 6.4 reshape.217
  73.1 6.4 fusion.40
  83.0 4.7 copy.72
  108.2 42.3 %all-gather.17.cloned.1.call-done = bf16[768,3072]{1,0:T(8,128)(2,1)} async-done(((bf16[384,3072]{1,0:T(8,128)(2,1)}), bf16[768,3072]{1,0:T(8,128)(2,1)}) %all-gather.17.cloned.1.call-update) | async-done | bytes 4718608 | tf_op jit(solution)/shard_map/all_gather | solution.py:64
  150.5 7.4 fusion.35
  157.9 56.7 %all-gather.19.cloned.1.call-done = bf16[3072,768]{1,0:T(8,128)(2,1)} async-done(((bf16[1536,768]{1,0:T(8,128)(2,1)}), bf16[3072,768]{1,0:T(8,128)(2,1)}) %all-gather.19.cloned.1.call-update) | async-done | bytes 4718608 | tf_op jit(solution)/shard_map/all_gather | solution.py:66
  214.6 21.2 %fusion.37 = (bf16[3072]{0:T(1024)(128)(2,1)S(1)}, bf16[560,3072]{1,0:T(8,128)(2,1)S(1)}, f32[560,3072]{1,0:T(8,128)}) fusion(f32[560,3072]{1,0:T(8,128)} %fusion.35, f32[3072]{0:T(1024)S(1)} %bitcast.87, bf16[560,768]{1,0:T(8,128)(2,1)S(1)} %bitcast.83, bf16[3072,768]{1,0:T(8,128)(2,1)} %all-gather.19.cloned.1.call-done), kind=kOutput, calls=%fused_computation.109 | convolution fusion | flops 2769712128 | bytes 22800384 | tf_op jit(solution)/shard_map/dot_general | solution.py:129
  248.2 4.6 copy.58
  252.7 9.3 %multiply_reduce_fusion = (f32[2,12,280]{2,1,0:T(8,128)S(1)}, f32[2,12,280,280]{2,3,1,0:T(8,128)S(1)}) fusion(f32[2,12,280,280]{2,3,1,0:T(8,128)} %copy-done, f32[2,12,280]{2,1,0:T(8,128)S(1)} %log_add_fusion, pred[2,280]{1,0:T(4,128)(4,1)S(1)} %iota_compare_fusion, bf16[2,280,12,64]{1,3,2,0:T(8,128)(2,1)} %copy.58, bf16[2,280,1,12,64]{1,4,3,0,2:T(8,128)(2,1)} %copy.72), kind=kOutput, calls=%fused_computation.1 | convolution fusion | flops 250246080 | bytes 16827440 | tf_op jit(solution)/shard_map/plhd,pmhd->phlm/dot_general | solution.py:144
  272.7 5.4 copy.63
  278.1 8.0 %convert_element_type.195 = bf16[560,2304]{0,1:T(8,128)(2,1)} reshape(bf16[2,280,3,12,64]{1,0,4,3,2:T(2,128)(2,1)} %copy.63) | data formatting | bytes 5160960 | tf_op jit(solution)/shard_map/convert_element_type | solution.py:160
  286.1 6.4 convolution_convert_fusion.2
  293.9 7.8 %convolution_convert_fusion.1 = bf16[768,3072]{1,0:T(8,128)(2,1)} fusion(bf16[560,3072]{1,0:T(8,128)(2,1)} %copy-done.35, f32[560,768]{1,0:T(8,128)S(1)} %copy-done.3, f32[768]{0:T(1024)S(1)} %reshape.204, f32[768]{0:T(1024)S(1)} %reshape.203, f32[560]{0:T(1024)S(1)} %add_rsqrt_fusion, f32[560]{0:T(1024)S(1)} %broadcast_multiply_fusion.4), kind=kOutput, calls=%fused_computation.27 | convolution fusion | flops 2646921216 | bytes 9890176 | tf_op jit(solution)/shard_map/dot_general | solution.py:131
  301.8 6.7 multiply_convert_fusion.1
  310.3 5.8 convolution_convert_fusion
  319.3 4.3 all-gather.7
  324.0 7.4 fusion.36
  331.5 7.4 all-reduce.9
  339.4 3.9 add_convert_fusion.2
  343.4 6.1 add_convert_fusion.3
  349.5 54.1 %reduce-scatter.9.cloned.1.call-done = bf16[384,3072]{1,0:T(8,128)(2,1)} async-done(((bf16[768,3072]{1,0:T(8,128)(2,1)}), bf16[384,3072]{1,0:T(8,128)(2,1)}) %reduce-scatter.9.cloned.1.call-update) | async-done | bytes 2359312 | tf_op jit(solution)/shard_map/reduce_scatter | solution.py:211
  403.6 63.0 %reduce-scatter.11.cloned.1.call-done = bf16[1536,768]{1,0:T(8,128)(2,1)} async-done(((bf16[3072,768]{1,0:T(8,128)(2,1)}), bf16[1536,768]{1,0:T(8,128)(2,1)}) %reduce-scatter.11.cloned.1.call-update) | async-done | bytes 2359312 | tf_op jit(solution)/shard_map/reduce_scatter | solution.py:217
  466.6 300.4 %all-reduce.11 = (f32[384]{0:T(512)}, f32[384]{0:T(512)}, f32[384,2304]{1,0:T(8,128)}, f32[768]{0:T(1024)}, f32[384,768]{1,0:T(8,128)}, /*index=5*/f32[384]{0:T(...) all-reduce(f32[384]{0:T(512)S(1)} %dynamic-slice_convert_fusion.7, ...), channel_id=1, replica_groups=mesh['dp'=16,'fsdp'=2] {'dp'}, use_global_device_ids=true, to_apply=%region_13.14 | all-reduce | flops 3543552 | bytes 21270528 | tf_op jit(solution)/shard_map/psum | solution.py:224
  (173 shorter events, 58.9 us)
Async XLA Ops:
  7.2 54.8 %all-gather.13.cloned.1.call-start = ((), (), s32[]{:S(2)}) async-start(), calls=%async_computation.4 | async-start | bytes 5308416 | tf_op jit(solution)/shard_map/all_gather | solution.py:56
  7.9 8.2 %copy-start.26 = (bf16[384]{0:T(512)(128)(2,1)S(1)}, bf16[384]{0:T(512)(128)(2,1)}, u32[]{:S(2)}) copy-start(bf16[384]{0:T(512)(128)(2,1)} %param.19) | copy-start | bytes 2308
  8.0 12.6 %copy-start.27 = (bf16[384]{0:T(512)(128)(2,1)S(1)}, bf16[384]{0:T(512)(128)(2,1)}, u32[]{:S(2)}) copy-start(bf16[384]{0:T(512)(128)(2,1)} %param.23) | copy-start | bytes 2308
  8.0 17.0 %copy-start.28 = (bf16[384]{0:T(512)(128)(2,1)S(1)}, bf16[384]{0:T(512)(128)(2,1)}, u32[]{:S(2)}) copy-start(bf16[384]{0:T(512)(128)(2,1)} %param.24) | copy-start | bytes 2308
  8.0 21.4 %copy-start.29 = (bf16[384]{0:T(512)(128)(2,1)S(1)}, bf16[384]{0:T(512)(128)(2,1)}, u32[]{:S(2)}) copy-start(bf16[384]{0:T(512)(128)(2,1)} %param.25) | copy-start | bytes 2308
  8.0 25.8 %copy-start.24 = (bf16[768]{0:T(1024)(128)(2,1)S(1)}, bf16[768]{0:T(1024)(128)(2,1)}, u32[]{:S(2)}) copy-start(bf16[768]{0:T(1024)(128)(2,1)} %param.21) | copy-start | bytes 4612
  8.0 97.2 %all-gather.15.cloned.1.call-start = ((), (), s32[]{:S(2)}) async-start(), calls=%async_computation.5 | async-start | bytes 1769472 | tf_op jit(solution)/shard_map/all_gather | solution.py:58
  8.7 29.5 %copy-start.23 = (bf16[1536]{0:T(1024)(128)(2,1)S(1)}, bf16[1536]{0:T(1024)(128)(2,1)}, u32[]{:S(2)}) copy-start(bf16[1536]{0:T(1024)(128)(2,1)} %param.27) | copy-start | bytes 9220
  8.8 141.8 %all-gather.17.cloned.1.call-start = ((), (), s32[]{:S(2)}) async-start(), calls=%async_computation.6 | async-start | bytes 7077888 | tf_op jit(solution)/shard_map/all_gather | solution.py:64
  9.5 205.1 %all-gather.19.cloned.1.call-start = ((), (), s32[]{:S(2)}) async-start(), calls=%async_computation.7 | async-start | bytes 7077888 | tf_op jit(solution)/shard_map/all_gather | solution.py:66
  10.1 339.4 %reduce-scatter.7.cloned.1.call-start = ((), (), s32[]{:S(2)}) async-start(), calls=%async_computation.9 | async-start | bytes 1769472 | tf_op jit(solution)/shard_map/reduce_scatter | solution.py:199
  10.8 34.8 %copy-start.17 = (f32[560]{0:T(1024)}, f32[560]{0:T(1024)S(1)}, u32[]{:S(2)}) copy-start(f32[560]{0:T(1024)S(1)} %div.27) | copy-start | bytes 6724
  16.2 50.5 %copy-start.19 = (f32[768]{0:T(1024)}, f32[768]{0:T(1024)S(1)}, u32[]{:S(2)}) copy-start(f32[768]{0:T(1024)S(1)} %reshape.199) | copy-start | bytes 9220
  38.3 28.4 %copy-start.21 = (f32[560]{0:T(1024)}, f32[560]{0:T(1024)S(1)}, u32[]{:S(2)}) copy-start(f32[560]{0:T(1024)S(1)} %rsqrt.21) | copy-start | bytes 6724
  83.0 8.1 %copy-start.4 = (bf16[2,280,1,12,64]{1,4,3,0,2:T(8,128)(2,1)}, bf16[2,280,1,12,64]{1,4,3,0,2:T(8,128)(2,1)S(1)}, u32[]{:S(2)}) copy-start(bf16[2,280,1,12,64]{1,4,3,0,2:T(8,128)(2,1)S(1)} %copy.73) | copy-start | bytes 2580484
  94.1 4.9 copy-start
  94.2 4.9 copy-start.9
  107.6 131.5 %copy-start.2 = (f32[560,768]{1,0:T(8,128)}, f32[560,768]{1,0:T(8,128)S(1)}, u32[]{:S(2)}) copy-start(f32[560,768]{1,0:T(8,128)S(1)} %fusion.15) | copy-start | bytes 5160964
  108.2 106.4 %copy-start.11 = (bf16[2,280,768]{2,1,0:T(8,128)(2,1)S(1)}, bf16[2,280,768]{2,1,0:T(8,128)(2,1)}, u32[]{:S(2)}) copy-start(bf16[2,280,768]{2,1,0:T(8,128)(2,1)} %param.17) | copy-start | bytes 2580484
  214.6 21.2 %copy-start.31 = (bf16[768,3072]{1,0:T(8,128)(2,1)S(1)}, bf16[768,3072]{1,0:T(8,128)(2,1)}, u32[]{:S(2)}) copy-start(bf16[768,3072]{1,0:T(8,128)(2,1)} %all-gather.17.cloned.1.call-done) | copy-start | bytes 14155780
  243.2 106.3 %reduce-scatter.5.cloned.1.call-start = ((), (), s32[]{:S(2)}) async-start(), calls=%async_computation.8 | async-start | bytes 5308416 | tf_op jit(solution)/shard_map/reduce_scatter | solution.py:193
  248.2 13.9 %slice-start = ((s8[10321920]{0:T(1024)(128)(4,1)}), s8[1933312]{0:T(1024)(128)(4,1)S(1)}, s32[]{:S(2)}) async-start(s8[10321920]{0:T(1024)(128)(4,1)} %bitcast.81), calls=%async_computation.12 | async-start | bytes 3866624
  252.7 9.3 %slice-start.1 = ((s8[10321920]{0:T(1024)(128)(4,1)}), s8[4194304]{0:T(1024)(128)(4,1)S(1)}, s32[]{:S(2)}) async-start(s8[10321920]{0:T(1024)(128)(4,1)} %bitcast.81), calls=%async_computation.13 | async-start | bytes 8388608
  252.7 9.4 %slice-start.2 = ((s8[10321920]{0:T(1024)(128)(4,1)}), s8[4194304]{0:T(1024)(128)(4,1)S(1)}, s32[]{:S(2)}) async-start(s8[10321920]{0:T(1024)(128)(4,1)} %bitcast.81), calls=%async_computation.14 | async-start | bytes 8388608
  278.1 8.0 %copy-start.16 = (bf16[2,280,768]{2,1,0:T(8,128)(2,1)S(1)}, bf16[2,280,768]{2,1,0:T(8,128)(2,1)}, u32[]{:S(2)}) copy-start(bf16[2,280,768]{2,1,0:T(8,128)(2,1)} %fusion.13) | copy-start | bytes 2580484
  292.5 111.1 %reduce-scatter.9.cloned.1.call-start = ((), (), s32[]{:S(2)}) async-start(), calls=%async_computation.10 | async-start | bytes 7077888 | tf_op jit(solution)/shard_map/reduce_scatter | solution.py:211
  301.7 164.9 %reduce-scatter.11.cloned.1.call-start = ((), (), s32[]{:S(2)}) async-start(), calls=%async_computation.11 | async-start | bytes 7077888 | tf_op jit(solution)/shard_map/reduce_scatter | solution.py:217
  301.8 8.5 %copy-start.12 = (bf16[2,280,768]{2,1,0:T(8,128)(2,1)S(1)}, bf16[2,280,768]{2,1,0:T(8,128)(2,1)}, u32[]{:S(2)}) copy-start(bf16[2,280,768]{2,1,0:T(8,128)(2,1)} %param.17) | copy-start | bytes 2580484
  316.1 7.9 %copy-start.18 = (f32[560]{0:T(1024)S(1)}, f32[560]{0:T(1024)}, u32[]{:S(2)}) copy-start(f32[560]{0:T(1024)} %copy-done.17) | copy-start | bytes 6724
  316.1 7.9 %copy-start.20 = (f32[768]{0:T(1024)S(1)}, f32[768]{0:T(1024)}, u32[]{:S(2)}) copy-start(f32[768]{0:T(1024)} %copy-done.19) | copy-start | bytes 9220
  316.1 7.9 %copy-start.22 = (f32[560]{0:T(1024)S(1)}, f32[560]{0:T(1024)}, u32[]{:S(2)}) copy-start(f32[560]{0:T(1024)} %copy-done.21) | copy-start | bytes 6724
  338.8 4.6 copy-start.14
  (15 other events, 35.5 us)
Sparse Core Ops, SparseCore 0:
  9.6 52.3 all-gather.12
  63.5 22.7 all-gather.14
  87.8 62.6 all-gather.16
  151.9 62.6 all-gather.18
  243.3 21.7 reduce-scatter.6
  292.6 48.1 reduce-scatter.4
  343.7 59.9 reduce-scatter.8
  406.6 59.9 reduce-scatter.10
where the time goes:
time: 782 us; the launch traced here: 774 us
  blocking collectives  343 us (44%)
  waiting for transfers between devices  235 us (30%)
  matrix products  98 us (13%)
  local copies, waits for them, and re-layouts  56.6 us (7%)
  other arithmetic  23.4 us (3%)
  between operations  17.2 us (2%)
    psum x1, blocking collectives, on_device(): lax.psum((pieces[0], pieces[1], pieces[2], pieces[3], pieces[4], pieces[5...  300 us
    reduce_scatter x1, waiting for transfers between devices, on_device(): lax.psum_scatter(gradients[10].astype(jnp.bfloat16), 'fsdp', scatter_dime...  63 us
    all_gather x1, waiting for transfers between devices, on_device(): lax.all_gather(down_weight, 'fsdp', axis=0, tiled=True)  56.7 us
    reduce_scatter x1, waiting for transfers between devices, on_device(): lax.psum_scatter(gradients[8].astype(jnp.bfloat16), 'fsdp', scatter_dimen...  54.1 us
    all_gather x1, waiting for transfers between devices, on_device(): lax.all_gather(up_weight, 'fsdp', axis=0, tiled=True)  42.3 us
    dot_general x1, matrix products, on_device(): jnp.dot(grad_out_b, weight_down_back.T, preferred_element_type=f32)  21.2 us
    unnamed x90, local copies, waits for them, and re-layouts  19.7 us
    all_gather x1, waiting for transfers between devices, on_device(): lax.all_gather(qkv_weight, 'fsdp', axis=0, tiled=True)  16.3 us
  transfers between devices with their start and end apart: 8, of which 5 were waited for; matrix products, arithmetic and copies ran while one was open for 18% of the time, Pallas kernels for 0%

commit v1 on v0

v1 whole, which is shorter than its diff:
```python
import functools

import jax
import jax.numpy as jnp
from jax import lax
from jax.experimental import pallas as pl
from jax.experimental.pallas import tpu as pltpu
from jax.sharding import PartitionSpec as P

TEXT = 40
MESH = pl.DeviceIdType.MESH
BF16 = jnp.bfloat16
F32 = jnp.float32
EPS = 1e-06
NZ = 4
GROUP = 16
PAIRS = 2
LENGTH = 280
LPAD = 288
ROWS = PAIRS * LPAD
D = 768
FF = 3072
HALF = D // 2
NCH = 18
WINDOW = 3
PIECES = (
    [(0, 32 * j, 32) for j in range(3)]
    + [(1, 0, 96)]
    + [(2, 32 * j, 32) for j in range(3)]
    + [(3, 96 * j, 96) for j in range(4)]
)
SMALL = (1, 1, 2, 1, 1, 1, 4, 1)
G1, B1, QV, OB, G2, B2, UB, DB = 0, 1, 2, 4, 5, 6, 7, 11
CHAINED = tuple(range(10)) + (13, 14)


def dot(a, b):
    return jnp.dot(a, b, preferred_element_type=F32)


def dot_nt(a, b):
    return lax.dot_general(a, b, (((1,), (1,)), ((), ())), preferred_element_type=F32)


def dot_tn(a, b):
    return lax.dot_general(a, b, (((0,), (0,)), ((), ())), preferred_element_type=F32)


def mult(x, n):
    return x if isinstance(x, int) else pl.multiple_of(x, n)


def ds(start, size, n=None):
    return pl.ds(mult(start, n or size), size)


def places():
    d = lax.axis_index("dp")
    f = lax.axis_index("fsdp")
    core = lax.rem(d, 2)
    y = lax.rem(d // 2, 2)
    z = lax.rem(d // 4, NZ)
    base = d - lax.rem(d, GROUP)

    def at(zz, yy, cc):
        return base + zz * 4 + yy * 2 + cc

    peers = {
        "c": (at(z, y, 1 - core), f),
        "x": (d, 1 - f),
        "y": (at(z, 1 - y, core), f),
    }
    for k in range(1, NZ):
        peers["z%d" % k] = (at(lax.rem(z + k, NZ), y, core), f)
    return f, core, y, z, peers


def norm_parts(v):
    c = v - jnp.mean(v, axis=-1, keepdims=True)
    r = lax.rsqrt(jnp.mean(c * c, axis=-1, keepdims=True) + EPS)
    return c * r, r


def layer_kernel(
    counts, tok, cot, w0, w1, w2, w3, s_in,
    res, gtok, gdown, gup, gqo, gsmall,
    xs, dys, h, lt, qkv, o, lse, x1, gact, dact, dh, vec, smv,
    v0, v1, v2, v3,
    own, snd, ownd, sndd,
    cb, xb, yb, zb, stg, cbd, xbd, ybd, zbd, stgd, sacc, srecv,
    gxs, gys, gcs, lsem, csem, xsem, ysem, zsem, azsem, aysem, acsem, psem, ssem,
):
    f, core, y, z, peers = places()
    ins = (w0, w1, w2, w3)
    ws = (v0, v1, v2, v3)
    barrier = pltpu.get_barrier_semaphore()
    for name in peers:
        pl.semaphore_signal(barrier, inc=1, device_id=peers[name], device_id_type=MESH)

    def send(src, dst, sems, idx, name):
        return pltpu.make_async_remote_copy(
            src_ref=src, dst_ref=dst, send_sem=sems.at[(0,) + idx], recv_sem=sems.at[(1,) + idx],
            device_id=peers[name], device_id_type=MESH,
        )

    def piece(g, half, yy):
        w, r0, rows = PIECES[g]
        full = ins[w].shape[0]
        return w, pl.ds(pl.multiple_of(half * full + (core * 2 + yy) * (full // 4) + r0, 16), rows)

    def gx(g):
        w, there = piece(g, f, y)
        _, here = piece(g, 0, y)
        return send(ins[w].at[here], ws[w].at[there], gxs, (g,), "x")

    def gy(g):
        w, at = piece(g, 1 - f, y)
        return send(ws[w].at[at], ws[w].at[at], gys, (g,), "y")

    def gc(g, k):
        w, at = piece(g, 1 - f, y if k == 0 else 1 - y)
        return send(ws[w].at[at], ws[w].at[at], gcs, (g, k), "c")

    def got_x(g):
        gx(g).wait()
        if g + WINDOW < len(PIECES):
            gx(g + WINDOW).start()
        gy(g).start()
        gc(g, 0).start()

    def got_y(g):
        gy(g).wait()
        gc(g, 1).start()

    def got(g):
        gc(g, 0).wait()
        gc(g, 1).wait()

    local = []
    for i in range(4):
        full = ins[i].shape[0]
        local.append(pltpu.make_async_copy(ins[i], ws[i].at[pl.ds(pl.multiple_of(f * full, 16), full)], lsem.at[i]))
    local.append(pltpu.make_async_copy(s_in, smv.at[f], lsem.at[4]))
    for cp in local:
        cp.start()
    pl.semaphore_wait(barrier, len(peers))
    small_x = send(s_in, smv.at[f], ssem, (6,), "x")
    small_x.start()
    for g in range(WINDOW):
        gx(g).start()

    def c_copy(i, down):
        if down:
            return send(sndd.at[lax.rem(i, 2)], cbd.at[i], csem, (i,), "c")
        return send(snd.at[lax.rem(i, 2)], cb.at[i - 6], csem, (i,), "c")

    def x_copy(i):
        if i < 6:
            return send(cbd.at[i, 1 - f], xbd.at[i], xsem, (i,), "x")
        return send(cb.at[i - 6, 1 - f], xb.at[i - 6], xsem, (i,), "x")

    def bufs(i):
        if i < 6:
            return i, 128, D, cbd, xbd, ybd, zbd, stgd
        return i - 6, HALF, 256, cb, xb, yb, zb, stg

    def y_copy(i):
        j, ur, uc, _, xx, yy, _, _ = bufs(i)
        return send(xx.at[j, ds((1 - y) * (ur // 2), ur // 2)], yy.at[j], ysem, (i,), "y")

    def z_copy(i, k):
        j, ur, uc, _, _, yy, zz, _ = bufs(i)
        return send(
            yy.at[j, ds(lax.rem(z + k, NZ) * (ur // 8), ur // 8)], zz.at[j, k - 1], zsem, (i, k - 1), "z%d" % k
        )

    def outpart(i, start, rows):
        j = i % 6 if i < 12 else (i - 12 + 5) % 6
        if i < 6:
            return gdown.at[pl.ds(pl.multiple_of((2 * j + core) * 128 + start, 16), rows), :]
        ref = gup if i < 12 else gqo
        return ref.at[pl.ds(mult(start, 16), rows), ds((2 * j + core) * 256, 256)]

    def own_piece(i):
        j, ur, uc, _, _, _, _, st = bufs(i)
        return outpart(i, y * (ur // 2) + z * (ur // 8), ur // 8), st.at[j]

    def p_copy(i):
        dst, src = own_piece(i)
        return pltpu.make_async_copy(src, dst, psem.at[i])

    def az_copy(i, k):
        dst, src = own_piece(i)
        return send(src, dst, azsem, (i, k - 1), "z%d" % k)

    def ay_copy(i):
        ur = 128 if i < 6 else HALF
        part = outpart(i, y * (ur // 2), ur // 2)
        return send(part, part, aysem, (i,), "y")

    def ac_copy(i):
        ur = 128 if i < 6 else HALF
        part = outpart(i, 0, ur)
        return send(part, part, acsem, (i,), "c")

    def s1(i, down):
        c_copy(i, down).wait()
        if down:
            cbd[i] = (cbd[i].astype(F32) + ownd[lax.rem(i, 2)].astype(F32)).astype(BF16)
        else:
            cb[i - 6] = (cb[i - 6].astype(F32) + own[lax.rem(i, 2)].astype(F32)).astype(BF16)

    def s2(i):
        x_copy(i).wait()
        if i in CHAINED:
            x_copy(i + WINDOW).start()
        j, ur, uc, cc, xx, _, _, _ = bufs(i)
        xx[j] = (xx[j].astype(F32) + cc[j, f].astype(F32)).astype(BF16)
        y_copy(i).start()

    def s3(i):
        y_copy(i).wait()
        j, ur, uc, _, xx, yy, _, _ = bufs(i)
        yy[j] = (yy[j].astype(F32) + xx[j, ds(y * (ur // 2), ur // 2)].astype(F32)).astype(BF16)
        for k in range(1, NZ):
            z_copy(i, k).start()

    def s4(i):
        for k in range(1, NZ):
            z_copy(i, k).wait()
        j, ur, uc, _, _, yy, zz, st = bufs(i)
        total = yy[j, ds(z * (ur // 8), ur // 8)].astype(F32)
        for k in range(1, NZ):
            total = total + zz[j, k - 1].astype(F32)
        st[j] = total.astype(BF16)
        p_copy(i).start()
        for k in range(1, NZ):
            az_copy(i, k).start()

    def s5(i):
        p_copy(i).wait()
        for k in range(1, NZ):
            az_copy(i, k).wait()
        ay_copy(i).start()

    def s6(i):
        ay_copy(i).wait()
        ac_copy(i).start()

    def s7(i):
        ac_copy(i).wait()

    def slot(k):
        for lag, stage in enumerate((s2, s3, s4, s5, s6, s7)):
            if 0 <= k - lag < NCH:
                stage(k - lag)

    for p in range(PAIRS):
        xs[p * LPAD : p * LPAD + LENGTH] = tok[p].astype(F32)
        xs[p * LPAD + LENGTH : (p + 1) * LPAD] = jnp.zeros((LPAD - LENGTH, D), F32)
        dys[p * LPAD : (p + 1) * LPAD] = jnp.concatenate(
            [cot[p].astype(F32), jnp.zeros((LPAD - LENGTH, D), F32)], axis=0
        ).astype(BF16)

    local[4].wait()
    small_x.wait()
    s0 = smv[0].astype(F32)
    s1v = smv[1].astype(F32)
    for j, r in enumerate((G1, B1, OB, G2, B2, DB)):
        vec[j] = jnp.concatenate([s0[r : r + 1], s1v[r : r + 1]], axis=1)
    vec[6] = jnp.concatenate([s0[QV : QV + 1], s0[QV + 1 : QV + 2]], axis=1)
    vec[7] = jnp.zeros((1, D), F32)
    vec[8] = jnp.concatenate([s1v[QV : QV + 1], s1v[QV + 1 : QV + 2]], axis=1)
    vec[9] = jnp.concatenate([s0[UB : UB + 1], s0[UB + 1 : UB + 2]], axis=1)
    vec[10] = jnp.concatenate([s0[UB + 2 : UB + 3], s0[UB + 3 : UB + 4]], axis=1)
    vec[11] = jnp.concatenate([s1v[UB : UB + 1], s1v[UB + 1 : UB + 2]], axis=1)
    vec[12] = jnp.concatenate([s1v[UB + 2 : UB + 3], s1v[UB + 3 : UB + 4]], axis=1)

    def loop(n, body):
        def step(i, carry):
            body(i)
            return carry

        lax.fori_loop(0, n, step, 0)

    def transpose_into(src, k):
        def body(j):
            cols = ds(j * 128, 128)
            lt[k, cols, :] = src[:, cols].astype(F32).T.astype(BF16)

        loop(D // 128, body)

    def ln1(i):
        rows = ds(i * 96, 96)
        n, _ = norm_parts(xs[rows])
        h[rows] = (n * vec[0] + vec[1]).astype(BF16)

    loop(6, ln1)
    got_x(0)
    transpose_into(h, 0)
    got_x(1)
    got_y(0)
    got_x(2)
    got_y(1)
    got_x(3)
    got_y(2)
    for g in range(3):
        got(g)
    local[0].wait()

    def qkv_body(i):
        cols = ds(i * D, D)
        qkv[:, cols] = (dot(h[...], v0[:, cols]) + vec[6 + i]).astype(BF16)

    loop(3, qkv_body)
    lane = lax.broadcasted_iota(jnp.int32, (1, 128), 1)
    low = lane < 64
    key = lax.broadcasted_iota(jnp.int32, (1, LPAD), 1)

    def attend(i):
        for when, todo in ((1, lambda: (got_x(4), got_y(3))), (4, lambda: (got_x(5), got_y(4))), (7, lambda: (got_x(6), got_y(5))), (10, lambda: (got_x(7), got_y(6)))):
            pl.when(i == when)(lambda todo=todo: (todo(), None)[1])
        p = i // 6
        hp = lax.rem(i, 6)
        rows = ds(p * LPAD, LPAD)
        q = qkv[rows, ds(hp * 128, 128)].astype(F32) * 0.125
        k = qkv[rows, ds(D + hp * 128, 128)]
        v = qkv[rows, ds(2 * D + hp * 128, 128)]
        valid = key < TEXT + counts[p]
        outs = []
        ls = lse[rows]
        for e in range(2):
            qm = jnp.where(low if e == 0 else jnp.logical_not(low), q, 0.0).astype(BF16)
            s = jnp.where(valid, dot_nt(qm, k), -1e30)
            m = jnp.max(s, axis=-1, keepdims=True)
            ex = jnp.exp(s - m)
            t = jnp.sum(ex, axis=-1, keepdims=True)
            ls = jnp.where(lane == 2 * hp + e, m + jnp.log(t), ls)
            outs.append(dot((ex / t).astype(BF16), v))
        lse[rows] = ls
        o[rows, ds(hp * 128, 128)] = jnp.where(low, outs[0], outs[1]).astype(BF16)

    loop(12, attend)
    got(3)
    local[1].wait()

    def proj(i):
        cols = ds(i * 256, 256)
        x1[:, cols] = xs[:, cols] + dot(o[...], v1[:, cols]) + vec[2, :, cols]

    loop(3, proj)
    got_y(7)

    def ln2(i):
        rows = ds(i * 96, 96)
        n, _ = norm_parts(x1[rows])
        h[rows] = (n * vec[3] + vec[4]).astype(BF16)

    loop(6, ln2)
    got_x(8)
    transpose_into(o, 1)
    transpose_into(h, 2)
    for g in range(4, 7):
        got(g)
    local[2].wait()

    def up_tile(j):
        cols = ds(j * 256, 256)
        u = dot(h[...], v2[:, cols]) + vec[9 + j // 3, :, ds(lax.rem(j, 3) * 256, 256)]
        phi = 0.5 * (1.0 + lax.erf(u * 0.7071067811865476))
        gact[:, cols] = (u * phi).astype(BF16)
        dact[:, cols] = (phi + u * (0.3989422804014327 * jnp.exp(-0.5 * u * u))).astype(BF16)

    def down_chunk(i):
        par = lax.rem(i, 2)
        for x in range(2):
            cols = x * (FF // 2) + i * 256
            mine = gact[:, ds(cols + core * 128, 128)]
            other = gact[:, ds(cols + (1 - core) * 128, 128)]
            both = jnp.concatenate([mine, other], axis=1)
            for n in range(3):
                r = dot_tn(both, dys[:, n * 256 : (n + 1) * 256]).astype(BF16)
                ownd[par, x, :, n * 256 : (n + 1) * 256] = r[:128]
                sndd[par, x, :, n * 256 : (n + 1) * 256] = r[128:]
        c_copy(i, True).start()

    def phase_a(i):
        up_tile(i)
        up_tile(6 + i)
        down_chunk(i)

        @pl.when(i > 0)
        def _():
            s1(i - 1, True)

        for when, todo in (
            (0, lambda: (got_x(9), got_y(8))),
            (1, lambda: (got_x(10), got_y(9), x_copy(0).start())),
            (2, lambda: (got_y(10), x_copy(1).start())),
            (3, lambda: x_copy(2).start()),
            (4, lambda: slot(0)),
            (5, lambda: slot(1)),
        ):
            pl.when(i == when)(lambda todo=todo: (todo(), None)[1])

    loop(6, phase_a)
    s1(5, True)
    for g in range(7, 11):
        got(g)
    local[3].wait()

    def down_proj(n):
        cols = ds(n * 256, 256)
        r = (x1[:, cols] + dot(gact[...], v3[:, cols]) + vec[5, :, cols])
        for p in range(PAIRS):
            res[p, :, cols] = r[p * LPAD : p * LPAD + LENGTH].astype(BF16)

    loop(3, down_proj)
    slot(2)

    def du_tile(j):
        cols = ds(j * 256, 256)
        du = (dot_nt(dys[...], v3[cols, :]) * dact[:, cols].astype(F32)).astype(BF16)
        dact[:, cols] = du
        sums = jnp.sum(du.astype(F32), axis=0, keepdims=True)
        for e in range(2):
            sacc[j // 6, 3 * UB + 2 * lax.rem(j, 6) + e] = sums[:, e * 128 : (e + 1) * 128]

    def col_chunk(i, j, sel, src):
        par = lax.rem(i, 2)
        for side, dst in ((core, own), (1 - core, snd)):
            u = 2 * j + side
            col_unit(dst, par, u, sel, src)
        c_copy(i, False).start()

    def col_unit(dst, par, u, sel, src):
        r = dot(lt[sel], src[:, ds(u * 256, 256)]).astype(BF16)
        dst[par, 0] = r[:HALF]
        dst[par, 1] = r[HALF:]

    def phase_c(j):
        du_tile(2 * j)
        du_tile(2 * j + 1)
        col_chunk(6 + j, j, 2, dact)

        @pl.when(j > 0)
        def _():
            s1(5 + j, False)

        for when, todo in ((2, lambda: slot(3)), (5, lambda: slot(4))):
            pl.when(j == when)(lambda todo=todo: (todo(), None)[1])

    loop(6, phase_c)
    s1(11, False)

    def dh2_tile(n):
        cols = ds(n * 256, 256)
        dh[:, cols] = dot_nt(dact[...], v2[cols, :])

    loop(3, dh2_tile)
    slot(5)
    zero = jnp.zeros((1, D), F32)

    def spread(x, r, v):
        for j in range(v.shape[1] // 128):
            sacc[x, 3 * r + j] = v[:, j * 128 : (j + 1) * 128]

    def put(r, v):
        spread(0, r, v[:, :HALF])
        spread(1, r, v[:, HALF:])

    def ln2_back(i, carry):
        a, b, c2, d2 = carry
        rows = ds(i * 96, 96)
        n, r = norm_parts(x1[rows])
        g = dh[rows]
        e = g * vec[3]
        dy = dys[rows].astype(F32)
        dx = dy + r * (
            e - jnp.mean(e, axis=-1, keepdims=True) - n * jnp.mean(e * n, axis=-1, keepdims=True)
        )
        x1[rows] = dx
        da = dx.astype(BF16)
        qkv[rows, 3 * D :] = da
        return (
            a + jnp.sum(g * n, axis=0, keepdims=True),
            b + jnp.sum(g, axis=0, keepdims=True),
            c2 + jnp.sum(da.astype(F32), axis=0, keepdims=True),
            d2 + jnp.sum(dy, axis=0, keepdims=True),
        )

    sums = lax.fori_loop(0, 6, ln2_back, (zero, zero, zero, zero))
    for r, v in zip((G2, B2, OB, DB), sums):
        put(r, v)

    col_chunk(12, 5 + core // 2, 1, qkv)

    def do_tile(n):
        cols = ds(n * 256, 256)
        o[:, cols] = dot_nt(qkv[:, 3 * D :], v1[cols, :]).astype(BF16)

    loop(3, do_tile)
    s1(12, False)
    slot(6)

    def attend_back(i):
        for when, todo in ((2, lambda: slot(7)), (5, lambda: slot(8)), (8, lambda: slot(9)), (11, lambda: slot(10))):
            pl.when(i == when)(lambda todo=todo: (todo(), None)[1])
        p = i // 6
        hp = lax.rem(i, 6)
        rows = ds(p * LPAD, LPAD)
        q = qkv[rows, ds(hp * 128, 128)]
        k = qkv[rows, ds(D + hp * 128, 128)]
        v = qkv[rows, ds(2 * D + hp * 128, 128)]
        g = o[rows, ds(hp * 128, 128)]
        qf = q.astype(F32) * 0.125
        gf = g.astype(F32)
        valid = key < TEXT + counts[p]
        ls = lse[rows]
        got3 = []
        for e in range(2):
            keep = low if e == 0 else jnp.logical_not(low)
            qm = jnp.where(keep, qf, 0.0).astype(BF16)
            gm = jnp.where(keep, gf, 0.0).astype(BF16)
            total = jnp.sum(jnp.where(lane == 2 * hp + e, ls, 0.0), axis=-1, keepdims=True)
            pr = jnp.where(valid, jnp.exp(dot_nt(qm, k) - total), 0.0)
            dp = dot_nt(gm, v)
            dsc = (pr * (dp - jnp.sum(pr * dp, axis=-1, keepdims=True))).astype(BF16)
            got3.append((dot(dsc, k), dot_tn(dsc, q), dot_tn(pr.astype(BF16), g)))
        for part, scale in ((0, 0.125), (1, 0.125), (2, 1.0)):
            r = jnp.where(low, got3[0][part], got3[1][part]) * scale
            qkv[rows, ds(part * D + hp * 128, 128)] = r.astype(BF16)

    loop(12, attend_back)

    def phase_g(t):
        j = t + 1
        col_chunk(12 + j, t, 0, qkv)

        @pl.when(t > 0)
        def _():
            s1(11 + j, False)

        for when, todo in (
            (1, lambda: x_copy(13).start()),
            (2, lambda: (slot(11), x_copy(14).start())),
            (3, lambda: x_copy(15).start()),
        ):
            pl.when(t == when)(lambda todo=todo: (todo(), None)[1])

    loop(4, phase_g)
    for c in range(2):

        @pl.when(core == c)
        def _():
            for side, dst in ((c, own), (1 - c, snd)):
                col_unit(dst, 1, 8 + side, side, qkv)

    c_copy(17, False).start()
    s1(16, False)
    slot(12)
    s1(17, False)

    def dh1_tile(n):
        cols = ds(n * 256, 256)
        dh[:, cols] = dot_nt(qkv[:, : 3 * D], v0[cols, :])

    loop(3, dh1_tile)
    slot(13)

    def ln1_back(i, carry):
        a, b, qs, vs = carry
        rows = ds(i * 96, 96)
        n, r = norm_parts(xs[rows])
        g = dh[rows]
        e = g * vec[0]
        xs[rows] = x1[rows] + r * (
            e - jnp.mean(e, axis=-1, keepdims=True) - n * jnp.mean(e * n, axis=-1, keepdims=True)
        )
        return (
            a + jnp.sum(g * n, axis=0, keepdims=True),
            b + jnp.sum(g, axis=0, keepdims=True),
            qs + jnp.sum(qkv[rows, :D].astype(F32), axis=0, keepdims=True),
            vs + jnp.sum(qkv[rows, 2 * D : 3 * D].astype(F32), axis=0, keepdims=True),
        )

    ga, gb, qs, vs = lax.fori_loop(0, 6, ln1_back, (zero, zero, zero, zero))
    put(G1, ga)
    put(B1, gb)
    for x, v in ((0, qs), (1, vs)):
        spread(x, QV, v)
    for p in range(PAIRS):
        gtok[p] = xs[p * LPAD : p * LPAD + LENGTH].astype(BF16)

    k = 14
    for j, name in enumerate(("c", "x", "y")):
        cp = send(sacc, srecv.at[j], ssem, (j,), name)
        cp.start()
        slot(k)
        k += 1
        cp.wait()
        sacc[...] = sacc[...] + srecv[j]
    copies = [send(sacc, srecv.at[3 + z], ssem, (2 + k2,), "z%d" % k2) for k2 in range(1, NZ)]
    for cp in copies:
        cp.start()
    srecv[3 + z] = sacc[...]
    slot(k)
    k += 1
    for cp in copies:
        cp.wait()
    gsmall[...] = (srecv[3, f] + srecv[4, f]) + (srecv[5, f] + srecv[6, f])
    while k < NCH + 5:
        slot(k)
        k += 1


def layer(*arrays):
    vm = pltpu.VMEM
    dma = pltpu.SemaphoreType.DMA
    any_ = pl.BlockSpec(memory_space=pl.ANY)
    inside = pl.BlockSpec(memory_space=pltpu.VMEM)
    pieces = len(PIECES)
    return pl.pallas_call(
        layer_kernel,
        out_shape=[
            jax.ShapeDtypeStruct((PAIRS, LENGTH, D), BF16),
            jax.ShapeDtypeStruct((PAIRS, LENGTH, D), BF16),
            jax.ShapeDtypeStruct((FF // 2, D), BF16),
            jax.ShapeDtypeStruct((HALF, FF), BF16),
            jax.ShapeDtypeStruct((HALF, FF), BF16),
            jax.ShapeDtypeStruct((36, 1, 128), F32),
        ],
        in_specs=[pl.BlockSpec(memory_space=pltpu.SMEM), inside, inside] + [any_] * 5,
        out_specs=[inside, inside, any_, any_, any_, inside],
        scratch_shapes=[
            vm((ROWS, D), F32),
            vm((ROWS, D), BF16),
            vm((ROWS, D), BF16),
            vm((3, D, ROWS), BF16),
            vm((ROWS, 4 * D), BF16),
            vm((ROWS, D), BF16),
            vm((ROWS, 128), F32),
            vm((ROWS, D), F32),
            vm((ROWS, FF), BF16),
            vm((ROWS, FF), BF16),
            vm((ROWS, D), F32),
            vm((13, 1, D), F32),
            vm((2, 16, HALF), BF16),
            vm((D, 3 * D), BF16),
            vm((D, D), BF16),
            vm((D, FF), BF16),
            vm((FF, D), BF16),
            vm((2, 2, HALF, 256), BF16),
            vm((2, 2, HALF, 256), BF16),
            vm((2, 2, 128, D), BF16),
            vm((2, 2, 128, D), BF16),
            vm((12, 2, HALF, 256), BF16),
            vm((12, HALF, 256), BF16),
            vm((12, HALF // 2, 256), BF16),
            vm((12, NZ - 1, HALF // 8, 256), BF16),
            vm((12, HALF // 8, 256), BF16),
            vm((6, 2, 128, D), BF16),
            vm((6, 128, D), BF16),
            vm((6, 64, D), BF16),
            vm((6, NZ - 1, 16, D), BF16),
            vm((6, 16, D), BF16),
            vm((2, 36, 1, 128), F32),
            vm((7, 2, 36, 1, 128), F32),
            dma((2, pieces)),
            dma((2, pieces)),
            dma((2, pieces, 2)),
            dma((5,)),
            dma((2, NCH)),
            dma((2, NCH)),
            dma((2, NCH)),
            dma((2, NCH, NZ - 1)),
            dma((2, NCH, NZ - 1)),
            dma((2, NCH)),
            dma((2, NCH)),
            dma((NCH,)),
            dma((2, 7)),
        ],
        compiler_params=pltpu.CompilerParams(
            collective_id=1, has_side_effects=True, vmem_limit_bytes=63 << 20
        ),
        name="layer",
    )(*arrays)


def on_device(extra, tokens, patch_counts, cotangent, norm1_gain, norm1_bias, qkv_weight, qv_bias,
              out_weight, out_bias, norm2_gain, norm2_bias, up_weight, up_bias, down_weight, down_bias):
    small = jnp.concatenate(
        [norm1_gain, norm1_bias, qv_bias, out_bias, norm2_gain, norm2_bias, up_bias, down_bias,
         jnp.zeros((4 * HALF,), BF16)]
    ).reshape(16, HALF)
    result, grad_tokens, gdown, gup, gqo, gsmall = layer(
        patch_counts, tokens, cotangent, qkv_weight, out_weight, up_weight, down_weight, small
    )
    grads = [g.astype(F32) for g in (gdown, gup, gqo[:, : 3 * D], gqo[:, 3 * D :])] + [gsmall]
    if extra is not None:
        grads = lax.psum(grads, "dp", axis_index_groups=extra)
    down, up, qkv, out, gsmall = grads
    parts, at = [], 0
    for count in SMALL:
        parts.append(gsmall[3 * at : 3 * (at + count)].reshape(-1))
        at += count
    return (
        result, grad_tokens, parts[0], parts[1], qkv, parts[2], out, parts[3],
        parts[4], parts[5], up, parts[6], down, parts[7],
    )


def solution(mesh):
    dp = mesh.shape["dp"]
    extra = None
    if dp > GROUP:
        extra = [[j + GROUP * i for i in range(dp // GROUP)] for j in range(GROUP)]
    row = P(("dp", "fsdp"), None, None)
    vec = P("fsdp")
    mat = P("fsdp", None)
    return jax.shard_map(
        functools.partial(on_device, extra),
        mesh=mesh,
        in_specs=(row, P(("dp", "fsdp")), row, vec, vec, mat, vec, mat, vec, vec, vec, mat, vec, mat, vec),
        out_specs=(row, row, vec, vec, mat, vec, mat, vec, vec, vec, mat, vec, mat, vec),
        check_vma=False,
    )
```

time: 782 us -> 200 us (0.26)
  blocking collectives: 343 us -> 0 us
  waiting for transfers between devices: 235 us -> 0 us
  Pallas kernels: 0 us -> 174 us
  matrix products: 98 us -> 0 us
  local copies, waits for them, and re-layouts: 56.6 us -> 13.5 us
  between operations: 17.2 us -> 0.67 us
  other arithmetic: 23.4 us -> 11.1 us
    psum x1 -> x0, blocking collectives: 300 us -> none  [on_device(): lax.psum((pieces[0], pieces[1], pieces[2], pieces[3], pieces[4], pieces[5...]
    pallas_call x0 -> x1, Pallas kernels: none -> 174 us  [layer(): pl.pallas_call(layer_kernel, out_shape=[jax.ShapeDtypeStruct((PAIRS, LENG...]
    reduce_scatter x4 -> x0, waiting for transfers between devices: 117 us -> none  [the longest x1 63 us: on_device(): lax.psum_scatter(gradients[10].astype(jnp.bfloat16), 'fsdp', scatter_dime...]
    all_gather x4 -> x0, waiting for transfers between devices: 115 us -> none  [the longest x1 56.7 us: on_device(): lax.all_gather(down_weight, 'fsdp', axis=0, tiled=True)]
    dot_general x18 -> x0, matrix products: 98 us -> none  [the longest x1 21.2 us: on_device(): jnp.dot(grad_out_b, weight_down_back.T, preferred_element_type=f32)]
    all_gather x8 -> x0, blocking collectives: 35.8 us -> none  [the longest x1 5.22 us: on_device(): lax.all_gather(norm1_gain, 'fsdp', axis=0, tiled=True)]
    reshape x4 -> x1, local copies, waits for them, and re-layouts: 15.4 us -> 0.61 us  [on_device(): small = jnp.concatenate([norm1_gain, norm1_bias, qv_bias, out_bias, norm2...]
    convert_element_type x9 -> x0, local copies, waits for them, and re-layouts: 14.7 us -> none  [the longest x2 13.5 us: on_device(): grad_packed = jnp.stack([grad_query, grad_keys, grad_values], axis=2).ast...]
  transfers between devices with their start and end apart: 8 -> 0, of which waited for: 5 -> 0; matrix products, arithmetic and copies ran while one was open for 18% -> 0% of each run, Pallas kernels for 0% -> 0%
where the time goes in v1:
time: 200 us
  Pallas kernels  174 us (87%)
  local copies, waits for them, and re-layouts  13.5 us (7%)
  other arithmetic  11.1 us (6%)
    pallas_call x1, Pallas kernels, layer(): pl.pallas_call(layer_kernel, out_shape=[jax.ShapeDtypeStruct((PAIRS, LENG...  174 us
    convert_element_type x4, other arithmetic, on_device(): g.astype(F32)  11.1 us
    unnamed x18, local copies, waits for them, and re-layouts  8.7 us

profile of v1, /device:TPU:0, one launch (start us, length us, event | category | flops | bytes accessed | tf_op | source)
XLA Modules:
  0.0 199.6 jit_solution(12188292183072647902)
XLA Ops:
  0.7 0.9 dynamic-update-slice
  1.5 0.9 dynamic-update-slice.1
  2.4 0.8 dynamic-update-slice.2
  3.2 0.9 dynamic-update-slice.3
  4.1 0.9 dynamic-update-slice.4
  5.0 0.9 dynamic-update-slice.5
  5.8 0.9 dynamic-update-slice.6
  6.7 0.9 dynamic-update-slice.7
  7.5 0.3 dynamic-update-slice.8
  7.8 0.6 reshape.55.s_in
  8.4 174.3 %layer.1 = (bf16[2,280,768]{2,1,0:T(8,128)(2,1)}, bf16[2,280,768]{2,1,0:T(8,128)(2,1)}, bf16[1536,768]{1,0:T(8,128)(2,1)}, bf16[384,3072]{1,0:T(8,128)(2,1)}, bf...) custom-call(s32[2]{0:T(128)} %counts.1, bf16[2,280,768]{2,1,0:T(8,128)(2,1)} %tok.1, bf16[2,280,768]{2,1,0:T(8,128)(2,1)} %cot.1, ...), custom_call_target="tpu_custom_call" | custom-call | tf_op jit(solution)/shard_map/layer/pallas_call | solution.py:623
  182.7 1.3 slice_reduce_fusion.1
  184.0 1.3 slice_reduce_fusion
  185.3 1.3 slice_reduce_fusion.2
  186.6 2.2 %slice_convert_fusion.1 = f32[384,768]{1,0:T(8,128)} fusion(bf16[384,3072]{1,0:T(8,128)(2,1)} %get-tuple-element.23), kind=kLoop, calls=%fused_computation.1 | loop fusion | flops 294912 | bytes 1769472 | tf_op jit(solution)/shard_map/convert_element_type | solution.py:699
  188.8 0.0 copy-start.1
  188.8 3.6 %slice_convert_fusion = f32[384,2304]{1,0:T(8,128)} fusion(bf16[384,3072]{1,0:T(8,128)(2,1)} %get-tuple-element.23), kind=kLoop, calls=%fused_computation | loop fusion | flops 884736 | bytes 5308416 | tf_op jit(solution)/shard_map/convert_element_type | solution.py:699
  192.4 0.0 copy-done.1
  192.4 0.0 copy-start
  192.4 2.8 %convert_element_type.14 = f32[384,3072]{1,0:T(8,128)} convert(bf16[384,3072]{1,0:T(8,128)(2,1)S(1)} %copy-done.1) | non-fusion elementwise | flops 1179648 | bytes 7077888 | tf_op jit(solution)/shard_map/convert_element_type | solution.py:699
  195.2 0.0 copy-done
  195.2 0.0 copy-start.3
  195.2 0.0 copy-start.2
  195.2 2.5 %convert_element_type.15 = f32[1536,768]{1,0:T(8,128)} convert(bf16[1536,768]{1,0:T(8,128)(2,1)S(1)} %copy-done) | non-fusion elementwise | flops 1179648 | bytes 7077888 | tf_op jit(solution)/shard_map/convert_element_type | solution.py:699
  197.8 0.0 copy-done.3
  197.8 0.9 copy.40
  198.7 0.0 copy-done.2
  198.7 0.9 copy.41
  (2 shorter events, 0.0 us)
Async XLA Ops:
  188.8 3.7 %copy-start.1 = (bf16[384,3072]{1,0:T(8,128)(2,1)S(1)}, bf16[384,3072]{1,0:T(8,128)(2,1)}, u32[]{:S(2)}) copy-start(bf16[384,3072]{1,0:T(8,128)(2,1)} %get-tuple-element.24) | copy-start | bytes 7077892
  192.4 2.8 %copy-start = (bf16[1536,768]{1,0:T(8,128)(2,1)S(1)}, bf16[1536,768]{1,0:T(8,128)(2,1)}, u32[]{:S(2)}) copy-start(bf16[1536,768]{1,0:T(8,128)(2,1)} %get-tuple-element.25) | copy-start | bytes 7077892
  195.2 2.6 %copy-start.3 = (bf16[2,280,768]{2,1,0:T(8,128)(2,1)S(1)}, bf16[2,280,768]{2,1,0:T(8,128)(2,1)}, u32[]{:S(2)}) copy-start(bf16[2,280,768]{2,1,0:T(8,128)(2,1)} %get-tuple-element.46) | copy-start | bytes 2580484
  195.2 3.5 %copy-start.2 = (bf16[2,280,768]{2,1,0:T(8,128)(2,1)S(1)}, bf16[2,280,768]{2,1,0:T(8,128)(2,1)}, u32[]{:S(2)}) copy-start(bf16[2,280,768]{2,1,0:T(8,128)(2,1)} %get-tuple-element.47) | copy-start | bytes 2580484

commit v2 on v1

--- a/solution.py
+++ b/solution.py
@@ -22,16 +22,49 @@
 FF = 3072
 HALF = D // 2
 NCH = 18
-WINDOW = 3
+GW = 3
 PIECES = (
-    [(0, 32 * j, 32) for j in range(3)]
-    + [(1, 0, 96)]
-    + [(2, 32 * j, 32) for j in range(3)]
-    + [(3, 96 * j, 96) for j in range(4)]
+    [(0, 16 * j, 16) for j in range(6)]
+    + [(3, 0, 96)]
+    + [(1, 48 * j, 48) for j in range(2)]
+    + [(2, 16 * j, 16) for j in range(6)]
 )
+SHARED = 6
+GLAG = 3
+GATHER_AT = ((9,), (10,), (11,), (12,), (), (13,), (), (14,), (15,), (16,), (17,), ())
 SMALL = (1, 1, 2, 1, 1, 1, 4, 1)
 G1, B1, QV, OB, G2, B2, UB, DB = 0, 1, 2, 4, 5, 6, 7, 11
-CHAINED = tuple(range(10)) + (13, 14)
+
+
+def plan():
+    points = list(POINTS)
+    points += [("Z%d" % n, NCH, n + 1) for n in range(points[-1][2], SLOTS)]
+    acts, done, started = {}, 0, 0
+    for name, ready, upto in points:
+        todo = acts[name] = []
+        while True:
+            ahead = AHEAD if done < NARROW else AHEAD_LAST
+            while started < min(2 * NCH, 2 * ready, done + ahead):
+                todo.append(("start", started))
+                started += 1
+            if done == upto:
+                break
+            assert done >= 2 * NCH or started > done
+            todo.append(("slot", done))
+            done += 1
+    return acts
+
+
+POINTS = (
+    ("A2", 1, 0), ("A3", 2, 1), ("A4", 3, 2), ("A5", 4, 3), ("B", 6, 5), ("C0", 6, 5), ("C1", 6, 6), ("C2", 7,
+    7), ("C3", 8, 8), ("C4", 9, 9), ("C5", 10, 9), ("D", 12, 10), ("E0", 12, 12), ("E", 13, 13), ("F0", 13,
+    13), ("F1", 13, 13), ("F2", 13, 14), ("F3", 13, 14), ("F4", 13, 15), ("F5", 13, 15), ("F6", 13, 16),
+    ("F7", 13, 17), ("F8", 13, 17), ("F9", 13, 18), ("F10", 13, 18), ("F11", 13, 19), ("G2", 14, 20), ("G3",
+    15, 21), ("G4", 16, 22), ("H", 18, 23), ("I", 18, 24),
+)
+SLOTS = 2 * NCH + 14
+AHEAD, AHEAD_LAST, NARROW = 6, 3, 24
+PLAN = plan()
 
 
 def dot(a, b):
@@ -84,11 +117,11 @@
 def layer_kernel(
     counts, tok, cot, w0, w1, w2, w3, s_in,
     res, gtok, gdown, gup, gqo, gsmall,
-    xs, dys, h, lt, qkv, o, lse, x1, gact, dact, dh, vec, smv,
+    tokv, cotv, xs, dys, h, lt, qkv, o, lse, x1, gact, dact, dh, vec, smv,
     v0, v1, v2, v3,
     own, snd, ownd, sndd,
     cb, xb, yb, zb, stg, cbd, xbd, ybd, zbd, stgd, sacc, srecv,
-    gxs, gys, gcs, lsem, csem, xsem, ysem, zsem, azsem, aysem, acsem, psem, ssem,
+    gxs, gys, gcs, gzs, gzcs, lsem, csem, xsem, ysem, zsem, azsem, aysem, acsem, psem, ssem,
 ):
     f, core, y, z, peers = places()
     ins = (w0, w1, w2, w3)
@@ -103,10 +136,15 @@
             device_id=peers[name], device_id_type=MESH,
         )
 
-    def piece(g, half, yy):
+    def piece(g, half, yy, zz=None):
         w, r0, rows = PIECES[g]
         full = ins[w].shape[0]
-        return w, pl.ds(pl.multiple_of(half * full + (core * 2 + yy) * (full // 4) + r0, 16), rows)
+        quarter = core * 2 + yy
+        if g == SHARED:
+            start = half * full + (z if zz is None else zz) * (full // 4) + quarter * rows
+        else:
+            start = half * full + quarter * (full // 4) + r0
+        return w, pl.ds(pl.multiple_of(start, 16), rows)
 
     def gx(g):
         w, there = piece(g, f, y)
@@ -121,48 +159,85 @@
         w, at = piece(g, 1 - f, y if k == 0 else 1 - y)
         return send(ws[w].at[at], ws[w].at[at], gcs, (g, k), "c")
 
+    def gz(e, k):
+        w, at = piece(SHARED, 1 - f, y if e == 0 else 1 - y)
+        return send(ws[w].at[at], ws[w].at[at], gzs, (e, k - 1), "z%d" % k)
+
+    def gzc(k):
+        start = (1 - f) * (FF // 2) + lax.rem(z + NZ - k, NZ) * (FF // 8) + core * (FF // 16)
+        at = pl.ds(pl.multiple_of(start, 16), FF // 16)
+        return send(v3.at[at], v3.at[at], gzcs, (k - 1,), "c")
+
     def got_x(g):
         gx(g).wait()
-        if g + WINDOW < len(PIECES):
-            gx(g + WINDOW).start()
+        if g + GW < len(PIECES):
+            gx(g + GW).start()
         gy(g).start()
         gc(g, 0).start()
+        if g == SHARED:
+            for k in range(1, NZ):
+                gz(0, k).start()
 
     def got_y(g):
         gy(g).wait()
         gc(g, 1).start()
-
-    def got(g):
-        gc(g, 0).wait()
-        gc(g, 1).wait()
-
+        if g == SHARED:
+            for k in range(1, NZ):
+                gz(1, k).start()
+
+    def got_xy(g):
+        if g < len(PIECES):
+            got_x(g)
+        if g >= GLAG:
+            got_y(g - GLAG)
+
+    def got_z(k):
+        gz(0, k).wait()
+        gz(1, k).wait()
+        gzc(k).start()
+
+    def got(w):
+        for g in range(len(PIECES)):
+            if PIECES[g][0] == w:
+                gc(g, 0).wait()
+                gc(g, 1).wait()
+        if w == 3:
+            for k in range(1, NZ):
+                gzc(k).wait()
+        local[w].wait()
+
+    rows_in = (pltpu.make_async_copy(tok, tokv, lsem.at[5]), pltpu.make_async_copy(cot, cotv, lsem.at[6]))
+    rows_in[0].start()
     local = []
     for i in range(4):
         full = ins[i].shape[0]
         local.append(pltpu.make_async_copy(ins[i], ws[i].at[pl.ds(pl.multiple_of(f * full, 16), full)], lsem.at[i]))
     local.append(pltpu.make_async_copy(s_in, smv.at[f], lsem.at[4]))
-    for cp in local:
-        cp.start()
+    local[4].start()
     pl.semaphore_wait(barrier, len(peers))
     small_x = send(s_in, smv.at[f], ssem, (6,), "x")
     small_x.start()
-    for g in range(WINDOW):
+    for g in range(GW):
         gx(g).start()
+    rows_in[1].start()
+    for i in range(4):
+        local[i].start()
 
     def c_copy(i, down):
         if down:
-            return send(sndd.at[lax.rem(i, 2)], cbd.at[i], csem, (i,), "c")
-        return send(snd.at[lax.rem(i, 2)], cb.at[i - 6], csem, (i,), "c")
-
-    def x_copy(i):
-        if i < 6:
-            return send(cbd.at[i, 1 - f], xbd.at[i], xsem, (i,), "x")
-        return send(cb.at[i - 6, 1 - f], xb.at[i - 6], xsem, (i,), "x")
+            return send(sndd.at[lax.rem(i, 3)], cbd.at[i], csem, (i,), "c")
+        return send(snd.at[lax.rem(i, 3)], cb.at[i - 6], csem, (i,), "c")
 
     def bufs(i):
         if i < 6:
             return i, 128, D, cbd, xbd, ybd, zbd, stgd
         return i - 6, HALF, 256, cb, xb, yb, zb, stg
+
+    def x_copy(n):
+        i, e = n // 2, n % 2
+        j, ur, uc, cc, xx, _, _, _ = bufs(i)
+        half = ds(((1 - y) if e == 0 else y) * (ur // 2), ur // 2)
+        return send(cc.at[j, 1 - f, half], xx.at[j, half], xsem, (i, e), "x")
 
     def y_copy(i):
         j, ur, uc, _, xx, yy, _, _ = bufs(i)
@@ -206,22 +281,24 @@
     def s1(i, down):
         c_copy(i, down).wait()
         if down:
-            cbd[i] = (cbd[i].astype(F32) + ownd[lax.rem(i, 2)].astype(F32)).astype(BF16)
+            cbd[i] = (cbd[i].astype(F32) + ownd[lax.rem(i, 3)].astype(F32)).astype(BF16)
         else:
-            cb[i - 6] = (cb[i - 6].astype(F32) + own[lax.rem(i, 2)].astype(F32)).astype(BF16)
-
-    def s2(i):
-        x_copy(i).wait()
-        if i in CHAINED:
-            x_copy(i + WINDOW).start()
-        j, ur, uc, cc, xx, _, _, _ = bufs(i)
-        xx[j] = (xx[j].astype(F32) + cc[j, f].astype(F32)).astype(BF16)
-        y_copy(i).start()
+            cb[i - 6] = (cb[i - 6].astype(F32) + own[lax.rem(i, 3)].astype(F32)).astype(BF16)
+
+    def s2(n):
+        x_copy(n).wait()
+        i = n // 2
+        if n % 2 == 0:
+            j, ur, uc, cc, xx, _, _, _ = bufs(i)
+            half = ds((1 - y) * (ur // 2), ur // 2)
+            xx[j, half] = (xx[j, half].astype(F32) + cc[j, f, half].astype(F32)).astype(BF16)
+            y_copy(i).start()
 
     def s3(i):
         y_copy(i).wait()
-        j, ur, uc, _, xx, yy, _, _ = bufs(i)
-        yy[j] = (yy[j].astype(F32) + xx[j, ds(y * (ur // 2), ur // 2)].astype(F32)).astype(BF16)
+        j, ur, uc, cc, xx, yy, _, _ = bufs(i)
+        half = ds(y * (ur // 2), ur // 2)
+        yy[j] = (yy[j].astype(F32) + (xx[j, half].astype(F32) + cc[j, f, half].astype(F32))).astype(BF16)
         for k in range(1, NZ):
             z_copy(i, k).start()
 
@@ -250,17 +327,24 @@
     def s7(i):
         ac_copy(i).wait()
 
-    def slot(k):
-        for lag, stage in enumerate((s2, s3, s4, s5, s6, s7)):
-            if 0 <= k - lag < NCH:
-                stage(k - lag)
-
+    def slot(n):
+        if n < 2 * NCH:
+            s2(n)
+        for lag, stage in ((3, s3), (6, s4), (9, s5), (12, s6), (15, s7)):
+            if (n - lag) % 2 == 0 and 0 <= (n - lag) // 2 < NCH:
+                stage((n - lag) // 2)
+
+    def point(name):
+        for what, n in PLAN[name]:
+            if what == "start":
+                x_copy(n).start()
+            else:
+                slot(n)
+
+    rows_in[0].wait()
     for p in range(PAIRS):
-        xs[p * LPAD : p * LPAD + LENGTH] = tok[p].astype(F32)
+        xs[p * LPAD : p * LPAD + LENGTH] = tokv[p].astype(F32)
         xs[p * LPAD + LENGTH : (p + 1) * LPAD] = jnp.zeros((LPAD - LENGTH, D), F32)
-        dys[p * LPAD : (p + 1) * LPAD] = jnp.concatenate(
-            [cot[p].astype(F32), jnp.zeros((LPAD - LENGTH, D), F32)], axis=0
-        ).astype(BF16)
 
     local[4].wait()
     small_x.wait()
@@ -296,17 +380,18 @@
         h[rows] = (n * vec[0] + vec[1]).astype(BF16)
 
     loop(6, ln1)
-    got_x(0)
+    got_xy(0)
+    got_xy(1)
     transpose_into(h, 0)
-    got_x(1)
-    got_y(0)
-    got_x(2)
-    got_y(1)
-    got_x(3)
-    got_y(2)
-    for g in range(3):
-        got(g)
-    local[0].wait()
+    got_xy(2)
+    rows_in[1].wait()
+    for p in range(PAIRS):
+        dys[p * LPAD : (p + 1) * LPAD] = jnp.concatenate(
+            [cotv[p].astype(F32), jnp.zeros((LPAD - LENGTH, D), F32)], axis=0
+        ).astype(BF16)
+    for g in range(3, 6 + GLAG):
+        got_xy(g)
+    got(0)
 
     def qkv_body(i):
         cols = ds(i * D, D)
@@ -318,8 +403,9 @@
     key = lax.broadcasted_iota(jnp.int32, (1, LPAD), 1)
 
     def attend(i):
-        for when, todo in ((1, lambda: (got_x(4), got_y(3))), (4, lambda: (got_x(5), got_y(4))), (7, lambda: (got_x(6), got_y(5))), (10, lambda: (got_x(7), got_y(6)))):
-            pl.when(i == when)(lambda todo=todo: (todo(), None)[1])
+        for when, gs in enumerate(GATHER_AT):
+            if gs:
+                pl.when(i == when)(lambda gs=gs: [got_xy(g) for g in gs] and None)
         p = i // 6
         hp = lax.rem(i, 6)
         rows = ds(p * LPAD, LPAD)
@@ -341,15 +427,13 @@
         o[rows, ds(hp * 128, 128)] = jnp.where(low, outs[0], outs[1]).astype(BF16)
 
     loop(12, attend)
-    got(3)
-    local[1].wait()
+    got(1)
 
     def proj(i):
         cols = ds(i * 256, 256)
         x1[:, cols] = xs[:, cols] + dot(o[...], v1[:, cols]) + vec[2, :, cols]
 
     loop(3, proj)
-    got_y(7)
 
     def ln2(i):
         rows = ds(i * 96, 96)
@@ -357,12 +441,9 @@
         h[rows] = (n * vec[3] + vec[4]).astype(BF16)
 
     loop(6, ln2)
-    got_x(8)
     transpose_into(o, 1)
     transpose_into(h, 2)
-    for g in range(4, 7):
-        got(g)
-    local[2].wait()
+    got(2)
 
     def up_tile(j):
         cols = ds(j * 256, 256)
@@ -372,7 +453,7 @@
         dact[:, cols] = (phi + u * (0.3989422804014327 * jnp.exp(-0.5 * u * u))).astype(BF16)
 
     def down_chunk(i):
-        par = lax.rem(i, 2)
+        par = lax.rem(i, 3)
         for x in range(2):
             cols = x * (FF // 2) + i * 256
             mine = gact[:, ds(cols + core * 128, 128)]
@@ -387,36 +468,32 @@
     def phase_a(i):
         up_tile(i)
         up_tile(6 + i)
+
+        @pl.when(i > 1)
+        def _():
+            s1(i - 2, True)
+
+        for when in range(2, 6):
+            pl.when(i == when)(functools.partial(point, "A%d" % when))
+        for k in range(1, NZ):
+            pl.when(i == k + 2)(functools.partial(got_z, k))
         down_chunk(i)
 
-        @pl.when(i > 0)
-        def _():
-            s1(i - 1, True)
-
-        for when, todo in (
-            (0, lambda: (got_x(9), got_y(8))),
-            (1, lambda: (got_x(10), got_y(9), x_copy(0).start())),
-            (2, lambda: (got_y(10), x_copy(1).start())),
-            (3, lambda: x_copy(2).start()),
-            (4, lambda: slot(0)),
-            (5, lambda: slot(1)),
-        ):
-            pl.when(i == when)(lambda todo=todo: (todo(), None)[1])
-
     loop(6, phase_a)
-    s1(5, True)
-    for g in range(7, 11):
-        got(g)
-    local[3].wait()
+    got(3)
 
     def down_proj(n):
         cols = ds(n * 256, 256)
         r = (x1[:, cols] + dot(gact[...], v3[:, cols]) + vec[5, :, cols])
         for p in range(PAIRS):
-            res[p, :, cols] = r[p * LPAD : p * LPAD + LENGTH].astype(BF16)
+            tokv[p, :, cols] = r[p * LPAD : p * LPAD + LENGTH].astype(BF16)
 
     loop(3, down_proj)
-    slot(2)
+    result_out = pltpu.make_async_copy(tokv, res, lsem.at[5])
+    result_out.start()
+    s1(4, True)
+    s1(5, True)
+    point("B")
 
     def du_tile(j):
         cols = ds(j * 256, 256)
@@ -427,7 +504,7 @@
             sacc[j // 6, 3 * UB + 2 * lax.rem(j, 6) + e] = sums[:, e * 128 : (e + 1) * 128]
 
     def col_chunk(i, j, sel, src):
-        par = lax.rem(i, 2)
+        par = lax.rem(i, 3)
         for side, dst in ((core, own), (1 - core, snd)):
             u = 2 * j + side
             col_unit(dst, par, u, sel, src)
@@ -441,24 +518,25 @@
     def phase_c(j):
         du_tile(2 * j)
         du_tile(2 * j + 1)
+
+        @pl.when(j > 1)
+        def _():
+            s1(4 + j, False)
+
+        for when in range(6):
+            pl.when(j == when)(functools.partial(point, "C%d" % when))
         col_chunk(6 + j, j, 2, dact)
 
-        @pl.when(j > 0)
-        def _():
-            s1(5 + j, False)
-
-        for when, todo in ((2, lambda: slot(3)), (5, lambda: slot(4))):
-            pl.when(j == when)(lambda todo=todo: (todo(), None)[1])
-
     loop(6, phase_c)
-    s1(11, False)
 
     def dh2_tile(n):
         cols = ds(n * 256, 256)
         dh[:, cols] = dot_nt(dact[...], v2[cols, :])
 
     loop(3, dh2_tile)
-    slot(5)
+    s1(10, False)
+    s1(11, False)
+    point("D")
     zero = jnp.zeros((1, D), F32)
 
     def spread(x, r, v):
@@ -495,17 +573,19 @@
 
     col_chunk(12, 5 + core // 2, 1, qkv)
 
+    point("E0")
+
     def do_tile(n):
         cols = ds(n * 256, 256)
         o[:, cols] = dot_nt(qkv[:, 3 * D :], v1[cols, :]).astype(BF16)
 
     loop(3, do_tile)
     s1(12, False)
-    slot(6)
+    point("E")
 
     def attend_back(i):
-        for when, todo in ((2, lambda: slot(7)), (5, lambda: slot(8)), (8, lambda: slot(9)), (11, lambda: slot(10))):
-            pl.when(i == when)(lambda todo=todo: (todo(), None)[1])
+        for when in range(12):
+            pl.when(i == when)(functools.partial(point, "F%d" % when))
         p = i // 6
         hp = lax.rem(i, 6)
         rows = ds(p * LPAD, LPAD)
@@ -534,19 +614,13 @@
     loop(12, attend_back)
 
     def phase_g(t):
-        j = t + 1
-        col_chunk(12 + j, t, 0, qkv)
-
-        @pl.when(t > 0)
+        @pl.when(t > 1)
         def _():
-            s1(11 + j, False)
-
-        for when, todo in (
-            (1, lambda: x_copy(13).start()),
-            (2, lambda: (slot(11), x_copy(14).start())),
-            (3, lambda: x_copy(15).start()),
-        ):
-            pl.when(t == when)(lambda todo=todo: (todo(), None)[1])
+            s1(11 + t, False)
+
+        for when in range(2, 4):
+            pl.when(t == when)(functools.partial(point, "G%d" % when))
+        col_chunk(13 + t, t, 0, qkv)
 
     loop(4, phase_g)
     for c in range(2):
@@ -554,19 +628,20 @@
         @pl.when(core == c)
         def _():
             for side, dst in ((c, own), (1 - c, snd)):
-                col_unit(dst, 1, 8 + side, side, qkv)
+                col_unit(dst, 17 % 3, 8 + side, side, qkv)
 
     c_copy(17, False).start()
-    s1(16, False)
-    slot(12)
-    s1(17, False)
+    s1(15, False)
+    point("G4")
 
     def dh1_tile(n):
         cols = ds(n * 256, 256)
         dh[:, cols] = dot_nt(qkv[:, : 3 * D], v0[cols, :])
 
     loop(3, dh1_tile)
-    slot(13)
+    s1(16, False)
+    s1(17, False)
+    point("H")
 
     def ln1_back(i, carry):
         a, b, qs, vs = carry
@@ -590,28 +665,35 @@
     for x, v in ((0, qs), (1, vs)):
         spread(x, QV, v)
     for p in range(PAIRS):
-        gtok[p] = xs[p * LPAD : p * LPAD + LENGTH].astype(BF16)
-
-    k = 14
+        cotv[p] = xs[p * LPAD : p * LPAD + LENGTH].astype(BF16)
+    grad_out = pltpu.make_async_copy(cotv, gtok, lsem.at[6])
+    grad_out.start()
+    point("I")
+
+    n = POINTS[-1][2]
     for j, name in enumerate(("c", "x", "y")):
         cp = send(sacc, srecv.at[j], ssem, (j,), name)
         cp.start()
-        slot(k)
-        k += 1
+        for _ in range(2):
+            point("Z%d" % n)
+            n += 1
         cp.wait()
         sacc[...] = sacc[...] + srecv[j]
-    copies = [send(sacc, srecv.at[3 + z], ssem, (2 + k2,), "z%d" % k2) for k2 in range(1, NZ)]
+    copies = [send(sacc, srecv.at[3 + z], ssem, (2 + k,), "z%d" % k) for k in range(1, NZ)]
     for cp in copies:
         cp.start()
     srecv[3 + z] = sacc[...]
-    slot(k)
-    k += 1
+    for _ in range(2):
+        point("Z%d" % n)
+        n += 1
     for cp in copies:
         cp.wait()
     gsmall[...] = (srecv[3, f] + srecv[4, f]) + (srecv[5, f] + srecv[6, f])
-    while k < NCH + 5:
-        slot(k)
-        k += 1
+    while n < SLOTS:
+        point("Z%d" % n)
+        n += 1
+    result_out.wait()
+    grad_out.wait()
 
 
 def layer(*arrays):
@@ -630,9 +712,11 @@
             jax.ShapeDtypeStruct((HALF, FF), BF16),
             jax.ShapeDtypeStruct((36, 1, 128), F32),
         ],
-        in_specs=[pl.BlockSpec(memory_space=pltpu.SMEM), inside, inside] + [any_] * 5,
-        out_specs=[inside, inside, any_, any_, any_, inside],
+        in_specs=[pl.BlockSpec(memory_space=pltpu.SMEM)] + [any_] * 7,
+        out_specs=[any_] * 5 + [inside],
         scratch_shapes=[
+            vm((PAIRS, LENGTH, D), BF16),
+            vm((PAIRS, LENGTH, D), BF16),
             vm((ROWS, D), F32),
             vm((ROWS, D), BF16),
             vm((ROWS, D), BF16),
@@ -650,10 +734,10 @@
             vm((D, D), BF16),
             vm((D, FF), BF16),
             vm((FF, D), BF16),
-            vm((2, 2, HALF, 256), BF16),
-            vm((2, 2, HALF, 256), BF16),
-            vm((2, 2, 128, D), BF16),
-            vm((2, 2, 128, D), BF16),
+            vm((3, 2, HALF, 256), BF16),
+            vm((3, 2, HALF, 256), BF16),
+            vm((3, 2, 128, D), BF16),
+            vm((3, 2, 128, D), BF16),
             vm((12, 2, HALF, 256), BF16),
             vm((12, HALF, 256), BF16),
             vm((12, HALF // 2, 256), BF16),
@@ -669,9 +753,11 @@
             dma((2, pieces)),
             dma((2, pieces)),
             dma((2, pieces, 2)),
-            dma((5,)),
+            dma((2, 2, NZ - 1)),
+            dma((2, NZ - 1)),
+            dma((7,)),
             dma((2, NCH)),
-            dma((2, NCH)),
+            dma((2, NCH, 2)),
             dma((2, NCH)),
             dma((2, NCH, NZ - 1)),
             dma((2, NCH, NZ - 1)),
@@ -687,23 +773,82 @@
     )(*arrays)
 
 
+def finish_kernel(gdown, gup, gqo, gsmall, res, gtok, down, up, qkv, out, res_out, gtok_out, *vectors):
+    down[...] = gdown[...].astype(F32)
+    up[...] = gup[...].astype(F32)
+    qkv[...] = gqo[:, : 3 * D].astype(F32)
+    out[...] = gqo[:, 3 * D :].astype(F32)
+    res_out[...] = res[...]
+    gtok_out[...] = gtok[...]
+
+    @pl.when(pl.program_id(0) == 0)
+    def _():
+        at = 0
+        for v in vectors:
+            n = v.shape[0] // 128
+            for j in range(n):
+                v[j * 128 : (j + 1) * 128] = gsmall[at + j, 0]
+            at += n
+
+
+def finish(gdown, gup, gqo, gsmall, res, gtok):
+    steps = 8
+    rows = PAIRS * LENGTH // 7
+
+    def cut(n, width):
+        return pl.BlockSpec((n, width), lambda i: (i, 0))
+
+    tokens = pl.BlockSpec((rows, D), lambda i: (jnp.minimum(i, 6), 0))
+    out = pl.pallas_call(
+        finish_kernel,
+        grid=(steps,),
+        out_shape=[
+            jax.ShapeDtypeStruct((FF // 2, D), F32),
+            jax.ShapeDtypeStruct((HALF, FF), F32),
+            jax.ShapeDtypeStruct((HALF, 3 * D), F32),
+            jax.ShapeDtypeStruct((HALF, D), F32),
+            jax.ShapeDtypeStruct((PAIRS * LENGTH, D), BF16),
+            jax.ShapeDtypeStruct((PAIRS * LENGTH, D), BF16),
+        ]
+        + [jax.ShapeDtypeStruct((n * HALF,), F32) for n in SMALL],
+        in_specs=[
+            cut(FF // 2 // steps, D),
+            cut(HALF // steps, FF),
+            cut(HALF // steps, FF),
+            pl.BlockSpec((36, 1, 128), lambda i: (0, 0, 0)),
+            tokens,
+            tokens,
+        ],
+        out_specs=[
+            cut(FF // 2 // steps, D),
+            cut(HALF // steps, FF),
+            cut(HALF // steps, 3 * D),
+            cut(HALF // steps, D),
+            tokens,
+            tokens,
+        ]
+        + [pl.BlockSpec((n * HALF,), lambda i: (0,)) for n in SMALL],
+        name="finish",
+    )(gdown, gup, gqo, gsmall, res.reshape(PAIRS * LENGTH, D), gtok.reshape(PAIRS * LENGTH, D))
+    return out
+
+
 def on_device(extra, tokens, patch_counts, cotangent, norm1_gain, norm1_bias, qkv_weight, qv_bias,
               out_weight, out_bias, norm2_gain, norm2_bias, up_weight, up_bias, down_weight, down_bias):
-    small = jnp.concatenate(
-        [norm1_gain, norm1_bias, qv_bias, out_bias, norm2_gain, norm2_bias, up_bias, down_bias,
-         jnp.zeros((4 * HALF,), BF16)]
-    ).reshape(16, HALF)
+    small, at = 0, 0
+    for v in (norm1_gain, norm1_bias, qv_bias, out_bias, norm2_gain, norm2_bias, up_bias, down_bias):
+        small = small + jnp.pad(v, (at, 16 * HALF - at - v.size))
+        at += v.size
+    small = small.reshape(16, HALF)
     result, grad_tokens, gdown, gup, gqo, gsmall = layer(
         patch_counts, tokens, cotangent, qkv_weight, out_weight, up_weight, down_weight, small
     )
-    grads = [g.astype(F32) for g in (gdown, gup, gqo[:, : 3 * D], gqo[:, 3 * D :])] + [gsmall]
+    down, up, qkv, out, result, grad_tokens, *parts = finish(gdown, gup, gqo, gsmall, result, grad_tokens)
+    grads = [down, up, qkv, out] + parts
     if extra is not None:
         grads = lax.psum(grads, "dp", axis_index_groups=extra)
-    down, up, qkv, out, gsmall = grads
-    parts, at = [], 0
-    for count in SMALL:
-        parts.append(gsmall[3 * at : 3 * (at + count)].reshape(-1))
-        at += count
+    down, up, qkv, out, *parts = grads
+    result, grad_tokens = (v.reshape(PAIRS, LENGTH, D) for v in (result, grad_tokens))
     return (
         result, grad_tokens, parts[0], parts[1], qkv, parts[2], out, parts[3],
         parts[4], parts[5], up, parts[6], down, parts[7],

time: 200 us -> 183 us (0.915)
  local copies, waits for them, and re-layouts: 13.5 us -> 0.61 us
  other arithmetic: 11.1 us -> 0.81 us
  Pallas kernels: 174 us -> 181 us
    convert_element_type x4 -> x0, other arithmetic: 11.1 us -> none  [on_device(): g.astype(F32)]
    pallas_call x0 -> x1, Pallas kernels: none -> 10.5 us  [finish(): pl.pallas_call(finish_kernel, grid=(steps,), out_shape=[jax.ShapeDtypeStr...]
    unnamed x18 -> x0, local copies, waits for them, and re-layouts: 8.7 us -> none
    pallas_call x1, Pallas kernels: 174 us -> 170 us  [layer(): pl.pallas_call(layer_kernel, out_shape=[jax.ShapeDtypeStruct((PAIRS, LENG...]
    slice x3 -> x0, local copies, waits for them, and re-layouts: 3.91 us -> none  [on_device(): parts.append(gsmall[3 * at:3 * (at + count)].reshape(-1))]
where the time goes in v2:
time: 183 us
  Pallas kernels  181 us (99%)
    pallas_call x1, Pallas kernels, layer(): pl.pallas_call(layer_kernel, out_shape=[jax.ShapeDtypeStruct((PAIRS, LENG...  170 us
    pallas_call x1, Pallas kernels, finish(): pl.pallas_call(finish_kernel, grid=(steps,), out_shape=[jax.ShapeDtypeStr...  10.5 us

profile of v2, /device:TPU:0, one launch (start us, length us, event | category | flops | bytes accessed | tf_op | source)
XLA Modules:
  0.0 182.8 jit_solution(12551445979712882051)
XLA Ops:
  0.6 0.8 pad_add_fusion
  1.5 0.6 reshape.43.s_in
  2.1 170.0 %layer.1 = (bf16[2,280,768]{2,1,0:T(8,128)(2,1)}, bf16[2,280,768]{2,1,0:T(8,128)(2,1)}, bf16[1536,768]{1,0:T(8,128)(2,1)}, bf16[384,3072]{1,0:T(8,128)(2,1)}, bf...) custom-call(s32[2]{0:T(128)} %counts.1, bf16[2,280,768]{2,1,0:T(8,128)(2,1)} %tok.1, bf16[2,280,768]{2,1,0:T(8,128)(2,1)} %cot.1, ...), custom_call_target="tpu_custom_call" | custom-call | tf_op jit(solution)/shard_map/layer/pallas_call | solution.py:705
  172.1 10.5 %finish.1 = (f32[1536,768]{1,0:T(8,128)}, f32[384,3072]{1,0:T(8,128)}, f32[384,2304]{1,0:T(8,128)}, f32[384,768]{1,0:T(8,128)}, bf16[560,768]{1,0:T(8,128)(2,1)}...) custom-call(bf16[1536,768]{1,0:T(8,128)(2,1)} %get-tuple-element.34., ...), custom_call_target="tpu_custom_call" | custom-call | tf_op jit(solution)/shard_map/finish/pallas_call | solution.py:802

commit v3 on v2

--- a/solution.py
+++ b/solution.py
@@ -22,16 +22,18 @@
 FF = 3072
 HALF = D // 2
 NCH = 18
-GW = 3
+GW = 5
 PIECES = (
-    [(0, 16 * j, 16) for j in range(6)]
-    + [(3, 0, 96)]
-    + [(1, 48 * j, 48) for j in range(2)]
-    + [(2, 16 * j, 16) for j in range(6)]
+    [(2, 4, 0, 96, FF // 2, FF // 8, 0, FF // 8)]
+    + [(0, j, 0, 96, k * D + j * 256, 256, 0, 0) for j in range(3) for k in range(3)]
+    + [(1, 3, 48 * j, 48, 0, D, 0, 0) for j in range(2)]
+    + [(2, 4, 0, 96, 384 * j, 384, 0, 0) for j in range(4)]
+    + [(3, 5, 0, 48, 0, D, 48, 0)]
+    + [(3, 5, 192 + 96 * j, 96, 0, D, 0, 0) for j in range(2)]
 )
-SHARED = 6
+SHARED = [g for g, p in enumerate(PIECES) if p[6] or p[7]]
 GLAG = 3
-GATHER_AT = ((9,), (10,), (11,), (12,), (), (13,), (), (14,), (15,), (16,), (17,), ())
+STEPS = len(PIECES) + GLAG
 SMALL = (1, 1, 2, 1, 1, 1, 4, 1)
 G1, B1, QV, OB, G2, B2, UB, DB = 0, 1, 2, 4, 5, 6, 7, 11
 
@@ -56,14 +58,14 @@
 
 
 POINTS = (
-    ("A2", 1, 0), ("A3", 2, 1), ("A4", 3, 2), ("A5", 4, 3), ("B", 6, 5), ("C0", 6, 5), ("C1", 6, 6), ("C2", 7,
-    7), ("C3", 8, 8), ("C4", 9, 9), ("C5", 10, 9), ("D", 12, 10), ("E0", 12, 12), ("E", 13, 13), ("F0", 13,
-    13), ("F1", 13, 13), ("F2", 13, 14), ("F3", 13, 14), ("F4", 13, 15), ("F5", 13, 15), ("F6", 13, 16),
-    ("F7", 13, 17), ("F8", 13, 17), ("F9", 13, 18), ("F10", 13, 18), ("F11", 13, 19), ("G2", 14, 20), ("G3",
-    15, 21), ("G4", 16, 22), ("H", 18, 23), ("I", 18, 24),
+    ("A2", 1, 0), ("A3", 2, 1), ("A4", 3, 2), ("A5", 4, 3), ("B", 6, 5), ("C0", 6, 6), ("C1", 6, 6), ("C2", 7,
+    7), ("C3", 8, 8), ("C4", 9, 9), ("C5", 10, 10), ("D", 12, 11), ("E0", 12, 12), ("E", 13, 13), ("F0", 13,
+    13), ("F1", 13, 14), ("F2", 13, 14), ("F3", 13, 15), ("F4", 13, 16), ("F5", 13, 16), ("F6", 13, 17),
+    ("F7", 13, 17), ("F8", 13, 18), ("F9", 13, 18), ("F10", 13, 19), ("F11", 13, 20), ("G2", 14, 21), ("G3",
+    15, 22), ("G4", 16, 23), ("H", 18, 24), ("I", 18, 25),
 )
-SLOTS = 2 * NCH + 14
-AHEAD, AHEAD_LAST, NARROW = 6, 3, 24
+SLOTS = 2 * NCH + 11
+AHEAD, AHEAD_LAST, NARROW = 6, 6, 24
 PLAN = plan()
 
 
@@ -121,7 +123,7 @@
     v0, v1, v2, v3,
     own, snd, ownd, sndd,
     cb, xb, yb, zb, stg, cbd, xbd, ybd, zbd, stgd, sacc, srecv,
-    gxs, gys, gcs, gzs, gzcs, lsem, csem, xsem, ysem, zsem, azsem, aysem, acsem, psem, ssem,
+    gxs, gys, gcs, gzs, gsent, lsem, csent, rsent, csem, xsem, ysem, zsem, azsem, aysem, acsem, psem, ssem,
 ):
     f, core, y, z, peers = places()
     ins = (w0, w1, w2, w3)
@@ -130,81 +132,76 @@
     for name in peers:
         pl.semaphore_signal(barrier, inc=1, device_id=peers[name], device_id_type=MESH)
 
-    def send(src, dst, sems, idx, name):
+    def send(src, dst, sent, arrived, name):
         return pltpu.make_async_remote_copy(
-            src_ref=src, dst_ref=dst, send_sem=sems.at[(0,) + idx], recv_sem=sems.at[(1,) + idx],
+            src_ref=src, dst_ref=dst, send_sem=sent, recv_sem=arrived,
             device_id=peers[name], device_id_type=MESH,
         )
 
     def piece(g, half, yy, zz=None):
-        w, r0, rows = PIECES[g]
+        w, _, r0, rows, c0, cols, zr, zc = PIECES[g]
         full = ins[w].shape[0]
-        quarter = core * 2 + yy
-        if g == SHARED:
-            start = half * full + (z if zz is None else zz) * (full // 4) + quarter * rows
-        else:
-            start = half * full + quarter * (full // 4) + r0
-        return w, pl.ds(pl.multiple_of(start, 16), rows)
+        zz = z if zz is None else zz
+        start = half * full + (core * 2 + yy) * (full // 4) + r0 + zz * zr
+        return w, (pl.ds(pl.multiple_of(start, 16), rows), ds(c0 + zz * zc, cols, 128))
+
+    def same(g, yy, zz, sent, arrived, name):
+        w, at = piece(g, 1 - f, yy, zz)
+        return send(ws[w].at[at], ws[w].at[at], sent, arrived, name)
 
     def gx(g):
         w, there = piece(g, f, y)
         _, here = piece(g, 0, y)
-        return send(ins[w].at[here], ws[w].at[there], gxs, (g,), "x")
+        return send(ins[w].at[here], ws[w].at[there], gsent.at[0], gxs.at[g], "x")
 
     def gy(g):
-        w, at = piece(g, 1 - f, y)
-        return send(ws[w].at[at], ws[w].at[at], gys, (g,), "y")
-
-    def gc(g, k):
-        w, at = piece(g, 1 - f, y if k == 0 else 1 - y)
-        return send(ws[w].at[at], ws[w].at[at], gcs, (g, k), "c")
-
-    def gz(e, k):
-        w, at = piece(SHARED, 1 - f, y if e == 0 else 1 - y)
-        return send(ws[w].at[at], ws[w].at[at], gzs, (e, k - 1), "z%d" % k)
-
-    def gzc(k):
-        start = (1 - f) * (FF // 2) + lax.rem(z + NZ - k, NZ) * (FF // 8) + core * (FF // 16)
-        at = pl.ds(pl.multiple_of(start, 16), FF // 16)
-        return send(v3.at[at], v3.at[at], gzcs, (k - 1,), "c")
+        return same(g, y, z, gsent.at[1], gys.at[g], "y")
+
+    def gc(g, e, k=0):
+        arrived = gcs.at[PIECES[g][1]]
+        return same(g, y if e == 0 else 1 - y, lax.rem(z + NZ - k, NZ), gsent.at[2], arrived, "c")
+
+    def gz(g, e, k):
+        return same(g, y if e == 0 else 1 - y, z, gsent.at[3], gzs.at[SHARED.index(g), k - 1, e], "z%d" % k)
 
     def got_x(g):
-        gx(g).wait()
+        gx(g).wait_recv()
         if g + GW < len(PIECES):
             gx(g + GW).start()
         gy(g).start()
         gc(g, 0).start()
-        if g == SHARED:
+        if g in SHARED:
             for k in range(1, NZ):
-                gz(0, k).start()
+                gz(g, 0, k).start()
 
     def got_y(g):
-        gy(g).wait()
+        gy(g).wait_recv()
         gc(g, 1).start()
-        if g == SHARED:
+        if g in SHARED:
             for k in range(1, NZ):
-                gz(1, k).start()
-
-    def got_xy(g):
-        if g < len(PIECES):
-            got_x(g)
-        if g >= GLAG:
-            got_y(g - GLAG)
-
-    def got_z(k):
-        gz(0, k).wait()
-        gz(1, k).wait()
-        gzc(k).start()
-
-    def got(w):
-        for g in range(len(PIECES)):
-            if PIECES[g][0] == w:
-                gc(g, 0).wait()
-                gc(g, 1).wait()
-        if w == 3:
-            for k in range(1, NZ):
-                gzc(k).wait()
-        local[w].wait()
+                gz(g, 1, k).start()
+
+    def step(n):
+        if n < len(PIECES):
+            got_x(n)
+        if n >= GLAG:
+            got_y(n - GLAG)
+
+    def steps(first, last):
+        for n in range(first, last + 1):
+            step(n)
+
+    def got_z(g, k):
+        for e in range(2):
+            gz(g, e, k).wait_recv()
+            gc(g, e, k).start()
+
+    def whole(sem, rows):
+        at = v3.at[pl.ds(0, rows)]
+        return send(at, at, sem, sem, "c")
+
+    def got(j):
+        whole(gcs.at[j], (192, 192, 192, 192, 768, 768)[j]).wait_recv()
 
     rows_in = (pltpu.make_async_copy(tok, tokv, lsem.at[5]), pltpu.make_async_copy(cot, cotv, lsem.at[6]))
     rows_in[0].start()
@@ -215,7 +212,7 @@
     local.append(pltpu.make_async_copy(s_in, smv.at[f], lsem.at[4]))
     local[4].start()
     pl.semaphore_wait(barrier, len(peers))
-    small_x = send(s_in, smv.at[f], ssem, (6,), "x")
+    small_x = send(s_in, smv.at[f], ssem.at[0, 6], ssem.at[1, 6], "x")
     small_x.start()
     for g in range(GW):
         gx(g).start()
@@ -225,8 +222,8 @@
 
     def c_copy(i, down):
         if down:
-            return send(sndd.at[lax.rem(i, 3)], cbd.at[i], csem, (i,), "c")
-        return send(snd.at[lax.rem(i, 3)], cb.at[i - 6], csem, (i,), "c")
+            return send(sndd.at[lax.rem(i, 3)], cbd.at[i], csent.at[lax.rem(i, 3)], csem.at[i], "c")
+        return send(snd.at[lax.rem(i, 3)], cb.at[i - 6], csent.at[3 + lax.rem(i, 3)], csem.at[i], "c")
 
     def bufs(i):
         if i < 6:
@@ -237,16 +234,16 @@
         i, e = n // 2, n % 2
         j, ur, uc, cc, xx, _, _, _ = bufs(i)
         half = ds(((1 - y) if e == 0 else y) * (ur // 2), ur // 2)
-        return send(cc.at[j, 1 - f, half], xx.at[j, half], xsem, (i, e), "x")
+        return send(cc.at[j, 1 - f, half], xx.at[j, half], rsent.at[0], xsem.at[n], "x")
 
     def y_copy(i):
         j, ur, uc, _, xx, yy, _, _ = bufs(i)
-        return send(xx.at[j, ds((1 - y) * (ur // 2), ur // 2)], yy.at[j], ysem, (i,), "y")
+        return send(xx.at[j, ds((1 - y) * (ur // 2), ur // 2)], yy.at[j], rsent.at[1], ysem.at[i], "y")
 
     def z_copy(i, k):
         j, ur, uc, _, _, yy, zz, _ = bufs(i)
         return send(
-            yy.at[j, ds(lax.rem(z + k, NZ) * (ur // 8), ur // 8)], zz.at[j, k - 1], zsem, (i, k - 1), "z%d" % k
+            yy.at[j, ds(lax.rem(z + k, NZ) * (ur // 8), ur // 8)], zz.at[j, k - 1], rsent.at[2], zsem.at[i], "z%d" % k
         )
 
     def outpart(i, start, rows):
@@ -266,17 +263,17 @@
 
     def az_copy(i, k):
         dst, src = own_piece(i)
-        return send(src, dst, azsem, (i, k - 1), "z%d" % k)
+        return send(src, dst, rsent.at[3], azsem.at[i], "z%d" % k)
 
     def ay_copy(i):
         ur = 128 if i < 6 else HALF
         part = outpart(i, y * (ur // 2), ur // 2)
-        return send(part, part, aysem, (i,), "y")
+        return send(part, part, rsent.at[4], aysem.at[i], "y")
 
     def ac_copy(i):
         ur = 128 if i < 6 else HALF
         part = outpart(i, 0, ur)
-        return send(part, part, acsem, (i,), "c")
+        return send(part, part, rsent.at[5], acsem.at[0], "c")
 
     def s1(i, down):
         c_copy(i, down).wait()
@@ -286,7 +283,7 @@
             cb[i - 6] = (cb[i - 6].astype(F32) + own[lax.rem(i, 3)].astype(F32)).astype(BF16)
 
     def s2(n):
-        x_copy(n).wait()
+        x_copy(n).wait_recv()
         i = n // 2
         if n % 2 == 0:
             j, ur, uc, cc, xx, _, _, _ = bufs(i)
@@ -295,7 +292,7 @@
             y_copy(i).start()
 
     def s3(i):
-        y_copy(i).wait()
+        y_copy(i).wait_recv()
         j, ur, uc, cc, xx, yy, _, _ = bufs(i)
         half = ds(y * (ur // 2), ur // 2)
         yy[j] = (yy[j].astype(F32) + (xx[j, half].astype(F32) + cc[j, f, half].astype(F32))).astype(BF16)
@@ -303,9 +300,8 @@
             z_copy(i, k).start()
 
     def s4(i):
-        for k in range(1, NZ):
-            z_copy(i, k).wait()
         j, ur, uc, _, _, yy, zz, st = bufs(i)
+        send(zz.at[j], zz.at[j], rsent.at[2], zsem.at[i], "z1").wait_recv()
         total = yy[j, ds(z * (ur // 8), ur // 8)].astype(F32)
         for k in range(1, NZ):
             total = total + zz[j, k - 1].astype(F32)
@@ -316,21 +312,18 @@
 
     def s5(i):
         p_copy(i).wait()
-        for k in range(1, NZ):
-            az_copy(i, k).wait()
+        j, _, _, _, _, _, zz, _ = bufs(i)
+        send(zz.at[j], zz.at[j], rsent.at[3], azsem.at[i], "z1").wait_recv()
         ay_copy(i).start()
 
     def s6(i):
-        ay_copy(i).wait()
+        ay_copy(i).wait_recv()
         ac_copy(i).start()
-
-    def s7(i):
-        ac_copy(i).wait()
 
     def slot(n):
         if n < 2 * NCH:
             s2(n)
-        for lag, stage in ((3, s3), (6, s4), (9, s5), (12, s6), (15, s7)):
+        for lag, stage in ((3, s3), (6, s4), (9, s5), (12, s6)):
             if (n - lag) % 2 == 0 and 0 <= (n - lag) // 2 < NCH:
                 stage((n - lag) // 2)
 
@@ -380,34 +373,25 @@
         h[rows] = (n * vec[0] + vec[1]).astype(BF16)
 
     loop(6, ln1)
-    got_xy(0)
-    got_xy(1)
+    steps(0, 1)
     transpose_into(h, 0)
-    got_xy(2)
+    steps(2, 3)
     rows_in[1].wait()
     for p in range(PAIRS):
         dys[p * LPAD : (p + 1) * LPAD] = jnp.concatenate(
             [cotv[p].astype(F32), jnp.zeros((LPAD - LENGTH, D), F32)], axis=0
         ).astype(BF16)
-    for g in range(3, 6 + GLAG):
-        got_xy(g)
-    got(0)
-
-    def qkv_body(i):
-        cols = ds(i * D, D)
-        qkv[:, cols] = (dot(h[...], v0[:, cols]) + vec[6 + i]).astype(BF16)
-
-    loop(3, qkv_body)
+    steps(4, 6)
+
+    def qkv_body(j, i):
+        cols = ds(i * D + j * 256, 256)
+        qkv[:, cols] = (dot(h[...], v0[:, cols]) + vec[6 + i, :, j * 256 : (j + 1) * 256]).astype(BF16)
+
     lane = lax.broadcasted_iota(jnp.int32, (1, 128), 1)
     low = lane < 64
     key = lax.broadcasted_iota(jnp.int32, (1, LPAD), 1)
 
-    def attend(i):
-        for when, gs in enumerate(GATHER_AT):
-            if gs:
-                pl.when(i == when)(lambda gs=gs: [got_xy(g) for g in gs] and None)
-        p = i // 6
-        hp = lax.rem(i, 6)
+    def attend(p, hp):
         rows = ds(p * LPAD, LPAD)
         q = qkv[rows, ds(hp * 128, 128)].astype(F32) * 0.125
         k = qkv[rows, ds(D + hp * 128, 128)]
@@ -422,18 +406,35 @@
             ex = jnp.exp(s - m)
             t = jnp.sum(ex, axis=-1, keepdims=True)
             ls = jnp.where(lane == 2 * hp + e, m + jnp.log(t), ls)
-            outs.append(dot((ex / t).astype(BF16), v))
+            outs.append(dot((ex * (1.0 / t)).astype(BF16), v))
         lse[rows] = ls
         o[rows, ds(hp * 128, 128)] = jnp.where(low, outs[0], outs[1]).astype(BF16)
 
-    loop(12, attend)
-    got(1)
+    local[0].wait()
+    for j in range(3):
+        if j:
+            step(6 + 3 * j)
+        got(j)
+        for i in range(3):
+            qkv_body(j, i)
+
+        def heads(i):
+            for n in range(2):
+                pl.when(i == n)(functools.partial(step, 7 + 3 * j + n))
+            for p in range(PAIRS):
+                attend(p, 2 * j + i)
+
+        loop(2, heads)
+    step(15)
+    got(3)
+    local[1].wait()
 
     def proj(i):
         cols = ds(i * 256, 256)
         x1[:, cols] = xs[:, cols] + dot(o[...], v1[:, cols]) + vec[2, :, cols]
 
     loop(3, proj)
+    steps(16, 17)
 
     def ln2(i):
         rows = ds(i * 96, 96)
@@ -441,9 +442,11 @@
         h[rows] = (n * vec[3] + vec[4]).astype(BF16)
 
     loop(6, ln2)
-    transpose_into(o, 1)
-    transpose_into(h, 2)
-    got(2)
+    step(18)
+    for k in range(1, NZ):
+        got_z(SHARED[0], k)
+    got(4)
+    local[2].wait()
 
     def up_tile(j):
         cols = ds(j * 256, 256)
@@ -467,6 +470,11 @@
 
     def phase_a(i):
         up_tile(i)
+        for when, ns in ((0, (19,)), (1, (20, 21)), (2, (22,))):
+            if ns[0] < STEPS:
+                pl.when(i == when)(functools.partial(steps, ns[0], min(ns[-1], STEPS - 1)))
+        for k in range(1, NZ):
+            pl.when(i == k + 2)(functools.partial(got_z, SHARED[1], k))
         up_tile(6 + i)
 
         @pl.when(i > 1)
@@ -475,12 +483,13 @@
 
         for when in range(2, 6):
             pl.when(i == when)(functools.partial(point, "A%d" % when))
-        for k in range(1, NZ):
-            pl.when(i == k + 2)(functools.partial(got_z, k))
         down_chunk(i)
 
     loop(6, phase_a)
-    got(3)
+    transpose_into(o, 1)
+    transpose_into(h, 2)
+    got(5)
+    local[3].wait()
 
     def down_proj(n):
         cols = ds(n * 256, 256)
@@ -672,14 +681,16 @@
 
     n = POINTS[-1][2]
     for j, name in enumerate(("c", "x", "y")):
-        cp = send(sacc, srecv.at[j], ssem, (j,), name)
+        cp = send(sacc, srecv.at[j], ssem.at[0, j], ssem.at[1, j], name)
         cp.start()
         for _ in range(2):
             point("Z%d" % n)
             n += 1
         cp.wait()
         sacc[...] = sacc[...] + srecv[j]
-    copies = [send(sacc, srecv.at[3 + z], ssem, (2 + k,), "z%d" % k) for k in range(1, NZ)]
+    copies = [
+        send(sacc, srecv.at[3 + z], ssem.at[0, 2 + k], ssem.at[1, 2 + k], "z%d" % k) for k in range(1, NZ)
+    ]
     for cp in copies:
         cp.start()
     srecv[3 + z] = sacc[...]
@@ -694,6 +705,11 @@
         n += 1
     result_out.wait()
     grad_out.wait()
+    whole(acsem.at[0], 2304).wait_recv()
+    for sem, rows in ((0, 864), (1, 864), (2, 2304), (3, 576)):
+        whole(gsent.at[sem], rows).wait_send()
+    for sem, rows in ((0, 2304), (1, 1152), (2, 864), (3, 864), (4, 1152), (5, 2304)):
+        whole(rsent.at[sem], rows).wait_send()
 
 
 def layer(*arrays):
@@ -750,19 +766,21 @@
             vm((6, 16, D), BF16),
             vm((2, 36, 1, 128), F32),
             vm((7, 2, 36, 1, 128), F32),
-            dma((2, pieces)),
-            dma((2, pieces)),
-            dma((2, pieces, 2)),
-            dma((2, 2, NZ - 1)),
-            dma((2, NZ - 1)),
+            dma((pieces,)),
+            dma((pieces,)),
+            dma((6,)),
+            dma((len(SHARED), NZ - 1, 2)),
+            dma((4,)),
             dma((7,)),
-            dma((2, NCH)),
-            dma((2, NCH, 2)),
-            dma((2, NCH)),
-            dma((2, NCH, NZ - 1)),
-            dma((2, NCH, NZ - 1)),
-            dma((2, NCH)),
-            dma((2, NCH)),
+            dma((6,)),
+            dma((6,)),
+            dma((NCH,)),
+            dma((2 * NCH,)),
+            dma((NCH,)),
+            dma((NCH,)),
+            dma((NCH,)),
+            dma((NCH,)),
+            dma((1,)),
             dma((NCH,)),
             dma((2, 7)),
         ],

time: 183 us -> 173 us (0.945)
  Pallas kernels: 181 us -> 171 us
    pallas_call x1, Pallas kernels: 170 us -> 160 us  [layer(): pl.pallas_call(layer_kernel, out_shape=[jax.ShapeDtypeStruct((PAIRS, LENG...]
where the time goes in v3:
time: 173 us
  Pallas kernels  171 us (99%)
    pallas_call x1, Pallas kernels, layer(): pl.pallas_call(layer_kernel, out_shape=[jax.ShapeDtypeStruct((PAIRS, LENG...  160 us
    pallas_call x1, Pallas kernels, finish(): pl.pallas_call(finish_kernel, grid=(steps,), out_shape=[jax.ShapeDtypeStr...  10.5 us

profile of v3, /device:TPU:0, one launch (start us, length us, event | category | flops | bytes accessed | tf_op | source)
XLA Modules:
  0.0 172.9 jit_solution(11789411708114236967)
XLA Ops:
  0.6 0.8 pad_add_fusion
  1.5 0.6 reshape.43.s_in
  2.1 160.2 %layer.1 = (bf16[2,280,768]{2,1,0:T(8,128)(2,1)}, bf16[2,280,768]{2,1,0:T(8,128)(2,1)}, bf16[1536,768]{1,0:T(8,128)(2,1)}, bf16[384,3072]{1,0:T(8,128)(2,1)}, bf...) custom-call(s32[2]{0:T(128)} %counts.1, bf16[2,280,768]{2,1,0:T(8,128)(2,1)} %tok.1, bf16[2,280,768]{2,1,0:T(8,128)(2,1)} %cot.1, ...), custom_call_target="tpu_custom_call" | custom-call | tf_op jit(solution)/shard_map/layer/pallas_call | solution.py:721
  162.2 10.5 %finish.1 = (f32[1536,768]{1,0:T(8,128)}, f32[384,3072]{1,0:T(8,128)}, f32[384,2304]{1,0:T(8,128)}, f32[384,768]{1,0:T(8,128)}, bf16[560,768]{1,0:T(8,128)(2,1)}...) custom-call(bf16[1536,768]{1,0:T(8,128)(2,1)} %get-tuple-element.34., ...), custom_call_target="tpu_custom_call" | custom-call | tf_op jit(solution)/shard_map/finish/pallas_call | solution.py:820

commit v4 on v3

--- a/solution.py
+++ b/solution.py
@@ -22,6 +22,9 @@
 FF = 3072
 HALF = D // 2
 NCH = 18
+SPLIT = 18
+PARTS = [(i, 0, None) for i in range(SPLIT)] + [(i, 128 * e, 128) for i in range(SPLIT, NCH) for e in range(2)]
+NP = len(PARTS)
 GW = 5
 PIECES = (
     [(2, 4, 0, 96, FF // 2, FF // 8, 0, FF // 8)]
@@ -46,26 +49,27 @@
         todo = acts[name] = []
         while True:
             ahead = AHEAD if done < NARROW else AHEAD_LAST
-            while started < min(2 * NCH, 2 * ready, done + ahead):
+            while started < min(2 * NP, 2 * BY[ready], done + ahead):
                 todo.append(("start", started))
                 started += 1
             if done == upto:
                 break
-            assert done >= 2 * NCH or started > done
+            assert done >= 2 * NP or started > done
             todo.append(("slot", done))
             done += 1
     return acts
 
 
 POINTS = (
-    ("A2", 1, 0), ("A3", 2, 1), ("A4", 3, 2), ("A5", 4, 3), ("B", 6, 5), ("C0", 6, 6), ("C1", 6, 6), ("C2", 7,
-    7), ("C3", 8, 8), ("C4", 9, 9), ("C5", 10, 10), ("D", 12, 11), ("E0", 12, 12), ("E", 13, 13), ("F0", 13,
-    13), ("F1", 13, 14), ("F2", 13, 14), ("F3", 13, 15), ("F4", 13, 16), ("F5", 13, 16), ("F6", 13, 17),
-    ("F7", 13, 17), ("F8", 13, 18), ("F9", 13, 18), ("F10", 13, 19), ("F11", 13, 20), ("G2", 14, 21), ("G3",
-    15, 22), ("G4", 16, 23), ("H", 18, 24), ("I", 18, 25),
+    ("A1", 1, 0), ("A2", 1, 0), ("A3", 2, 1), ("A4", 3, 2), ("A5", 4, 3), ("B", 6, 5), ("C0", 6, 6), ("C1", 6,
+    8), ("C2", 7, 9), ("C3", 8, 10), ("C4", 9, 11), ("C5", 10, 13), ("D", 12, 14), ("E0", 12, 15), ("E", 13,
+    17), ("F0", 13, 17), ("F1", 13, 17), ("F2", 13, 18), ("F3", 13, 18), ("F4", 13, 19), ("F5", 13, 20),
+    ("F6", 13, 20), ("F7", 13, 21), ("F8", 13, 22), ("F9", 13, 22), ("F10", 13, 23), ("F11", 13, 24), ("G2",
+    14, 25), ("G3", 15, 26), ("G4", 16, 26), ("H", 18, 27), ("I", 18, 29),
 )
-SLOTS = 2 * NCH + 11
-AHEAD, AHEAD_LAST, NARROW = 6, 6, 24
+SLOTS = 2 * NP + 11
+BY = [sum(p[0] < n for p in PARTS) for n in range(NCH + 1)]
+AHEAD, AHEAD_LAST, NARROW = 4, 4, 24
 PLAN = plan()
 
 
@@ -230,49 +234,61 @@
             return i, 128, D, cbd, xbd, ybd, zbd, stgd
         return i - 6, HALF, 256, cb, xb, yb, zb, stg
 
-    def x_copy(n):
-        i, e = n // 2, n % 2
-        j, ur, uc, cc, xx, _, _, _ = bufs(i)
+    def bufs(n):
+        i, c0, width = PARTS[n]
+        if i < 6:
+            j, ur, refs = i, 128, (cbd, xbd, ybd, zbd, stgd)
+        else:
+            j, ur, refs = i - 6, HALF, (cb, xb, yb, zb, stg)
+        if width is None:
+            return (ur,) + tuple(r.at[j] for r in refs)
+        at = pl.ds(c0, width)
+        cc, xx, yy, zz, st = refs
+        return ur, cc.at[j, :, :, at], xx.at[j, :, at], yy.at[j, :, at], zz.at[j, :, :, at], st.at[j, :, at]
+
+    def x_copy(h):
+        n, e = h // 2, h % 2
+        ur, cc, xx, _, _, _ = bufs(n)
         half = ds(((1 - y) if e == 0 else y) * (ur // 2), ur // 2)
-        return send(cc.at[j, 1 - f, half], xx.at[j, half], rsent.at[0], xsem.at[n], "x")
-
-    def y_copy(i):
-        j, ur, uc, _, xx, yy, _, _ = bufs(i)
-        return send(xx.at[j, ds((1 - y) * (ur // 2), ur // 2)], yy.at[j], rsent.at[1], ysem.at[i], "y")
-
-    def z_copy(i, k):
-        j, ur, uc, _, _, yy, zz, _ = bufs(i)
+        return send(cc.at[1 - f, half], xx.at[half], rsent.at[0], xsem.at[h], "x")
+
+    def y_copy(n):
+        ur, _, xx, yy, _, _ = bufs(n)
+        return send(xx.at[ds((1 - y) * (ur // 2), ur // 2)], yy, rsent.at[1], ysem.at[n], "y")
+
+    def z_copy(n, k):
+        ur, _, _, yy, zz, _ = bufs(n)
         return send(
-            yy.at[j, ds(lax.rem(z + k, NZ) * (ur // 8), ur // 8)], zz.at[j, k - 1], rsent.at[2], zsem.at[i], "z%d" % k
+            yy.at[ds(lax.rem(z + k, NZ) * (ur // 8), ur // 8)], zz.at[k - 1], rsent.at[2], zsem.at[n], "z%d" % k
         )
 
-    def outpart(i, start, rows):
+    def outpart(n, start, rows):
+        i, c0, width = PARTS[n]
         j = i % 6 if i < 12 else (i - 12 + 5) % 6
         if i < 6:
             return gdown.at[pl.ds(pl.multiple_of((2 * j + core) * 128 + start, 16), rows), :]
         ref = gup if i < 12 else gqo
-        return ref.at[pl.ds(mult(start, 16), rows), ds((2 * j + core) * 256, 256)]
-
-    def own_piece(i):
-        j, ur, uc, _, _, _, _, st = bufs(i)
-        return outpart(i, y * (ur // 2) + z * (ur // 8), ur // 8), st.at[j]
-
-    def p_copy(i):
-        dst, src = own_piece(i)
-        return pltpu.make_async_copy(src, dst, psem.at[i])
-
-    def az_copy(i, k):
-        dst, src = own_piece(i)
-        return send(src, dst, rsent.at[3], azsem.at[i], "z%d" % k)
-
-    def ay_copy(i):
-        ur = 128 if i < 6 else HALF
-        part = outpart(i, y * (ur // 2), ur // 2)
-        return send(part, part, rsent.at[4], aysem.at[i], "y")
-
-    def ac_copy(i):
-        ur = 128 if i < 6 else HALF
-        part = outpart(i, 0, ur)
+        return ref.at[pl.ds(mult(start, 16), rows), ds((2 * j + core) * 256 + c0, width or 256, 128)]
+
+    def own_piece(n):
+        ur, _, _, _, _, st = bufs(n)
+        return outpart(n, y * (ur // 2) + z * (ur // 8), ur // 8), st
+
+    def p_copy(n):
+        dst, src = own_piece(n)
+        return pltpu.make_async_copy(src, dst, psem.at[n])
+
+    def az_copy(n, k):
+        dst, src = own_piece(n)
+        return send(src, dst, rsent.at[3], azsem.at[n], "z%d" % k)
+
+    def ay_copy(n):
+        ur = bufs(n)[0]
+        part = outpart(n, y * (ur // 2), ur // 2)
+        return send(part, part, rsent.at[4], aysem.at[n], "y")
+
+    def ac_copy(n):
+        part = outpart(n, 0, bufs(n)[0])
         return send(part, part, rsent.at[5], acsem.at[0], "c")
 
     def s1(i, down):
@@ -282,49 +298,49 @@
         else:
             cb[i - 6] = (cb[i - 6].astype(F32) + own[lax.rem(i, 3)].astype(F32)).astype(BF16)
 
-    def s2(n):
-        x_copy(n).wait_recv()
-        i = n // 2
-        if n % 2 == 0:
-            j, ur, uc, cc, xx, _, _, _ = bufs(i)
+    def s2(h):
+        x_copy(h).wait_recv()
+        n = h // 2
+        if h % 2 == 0:
+            ur, cc, xx, _, _, _ = bufs(n)
             half = ds((1 - y) * (ur // 2), ur // 2)
-            xx[j, half] = (xx[j, half].astype(F32) + cc[j, f, half].astype(F32)).astype(BF16)
-            y_copy(i).start()
-
-    def s3(i):
-        y_copy(i).wait_recv()
-        j, ur, uc, cc, xx, yy, _, _ = bufs(i)
+            xx[half] = (xx[half].astype(F32) + cc[f, half].astype(F32)).astype(BF16)
+            y_copy(n).start()
+
+    def s3(n):
+        y_copy(n).wait_recv()
+        ur, cc, xx, yy, _, _ = bufs(n)
         half = ds(y * (ur // 2), ur // 2)
-        yy[j] = (yy[j].astype(F32) + (xx[j, half].astype(F32) + cc[j, f, half].astype(F32))).astype(BF16)
+        yy[...] = (yy[...].astype(F32) + (xx[half].astype(F32) + cc[f, half].astype(F32))).astype(BF16)
         for k in range(1, NZ):
-            z_copy(i, k).start()
-
-    def s4(i):
-        j, ur, uc, _, _, yy, zz, st = bufs(i)
-        send(zz.at[j], zz.at[j], rsent.at[2], zsem.at[i], "z1").wait_recv()
-        total = yy[j, ds(z * (ur // 8), ur // 8)].astype(F32)
+            z_copy(n, k).start()
+
+    def s4(n):
+        ur, _, _, yy, zz, st = bufs(n)
+        send(zz, zz, rsent.at[2], zsem.at[n], "z1").wait_recv()
+        total = yy[ds(z * (ur // 8), ur // 8)].astype(F32)
         for k in range(1, NZ):
-            total = total + zz[j, k - 1].astype(F32)
-        st[j] = total.astype(BF16)
-        p_copy(i).start()
+            total = total + zz[k - 1].astype(F32)
+        st[...] = total.astype(BF16)
+        p_copy(n).start()
         for k in range(1, NZ):
-            az_copy(i, k).start()
-
-    def s5(i):
-        p_copy(i).wait()
-        j, _, _, _, _, _, zz, _ = bufs(i)
-        send(zz.at[j], zz.at[j], rsent.at[3], azsem.at[i], "z1").wait_recv()
-        ay_copy(i).start()
-
-    def s6(i):
-        ay_copy(i).wait_recv()
-        ac_copy(i).start()
+            az_copy(n, k).start()
+
+    def s5(n):
+        p_copy(n).wait()
+        zz = bufs(n)[4]
+        send(zz, zz, rsent.at[3], azsem.at[n], "z1").wait_recv()
+        ay_copy(n).start()
+
+    def s6(n):
+        ay_copy(n).wait_recv()
+        ac_copy(n).start()
 
     def slot(n):
-        if n < 2 * NCH:
+        if n < 2 * NP:
             s2(n)
         for lag, stage in ((3, s3), (6, s4), (9, s5), (12, s6)):
-            if (n - lag) % 2 == 0 and 0 <= (n - lag) // 2 < NCH:
+            if (n - lag) % 2 == 0 and 0 <= (n - lag) // 2 < NP:
                 stage((n - lag) // 2)
 
     def point(name):
@@ -477,11 +493,15 @@
             pl.when(i == k + 2)(functools.partial(got_z, SHARED[1], k))
         up_tile(6 + i)
 
-        @pl.when(i > 1)
+        @pl.when(i == 1)
+        def _():
+            s1(0, True)
+
+        @pl.when(i > 2)
         def _():
             s1(i - 2, True)
 
-        for when in range(2, 6):
+        for when in range(1, 6):
             pl.when(i == when)(functools.partial(point, "A%d" % when))
         down_chunk(i)
 
@@ -775,13 +795,13 @@
             dma((6,)),
             dma((6,)),
             dma((NCH,)),
-            dma((2 * NCH,)),
-            dma((NCH,)),
-            dma((NCH,)),
-            dma((NCH,)),
-            dma((NCH,)),
+            dma((2 * NP,)),
+            dma((NP,)),
+            dma((NP,)),
+            dma((NP,)),
+            dma((NP,)),
             dma((1,)),
-            dma((NCH,)),
+            dma((NP,)),
             dma((2, 7)),
         ],
         compiler_params=pltpu.CompilerParams(
@@ -796,11 +816,11 @@
     up[...] = gup[...].astype(F32)
     qkv[...] = gqo[:, : 3 * D].astype(F32)
     out[...] = gqo[:, 3 * D :].astype(F32)
-    res_out[...] = res[...]
-    gtok_out[...] = gtok[...]
 
     @pl.when(pl.program_id(0) == 0)
     def _():
+        res_out[...] = res[...]
+        gtok_out[...] = gtok[...]
         at = 0
         for v in vectors:
             n = v.shape[0] // 128
@@ -810,13 +830,13 @@
 
 
 def finish(gdown, gup, gqo, gsmall, res, gtok):
-    steps = 8
-    rows = PAIRS * LENGTH // 7
+    steps = 3
+    rows = PAIRS * LENGTH
 
     def cut(n, width):
         return pl.BlockSpec((n, width), lambda i: (i, 0))
 
-    tokens = pl.BlockSpec((rows, D), lambda i: (jnp.minimum(i, 6), 0))
+    tokens = pl.BlockSpec((rows, D), lambda i: (0, 0))
     out = pl.pallas_call(
         finish_kernel,
         grid=(steps,),

time: 173 us -> 171 us (0.988)
  Pallas kernels: 171 us -> 168 us
where the time goes in v4:
time: 171 us; the launch traced here: 170 us
  Pallas kernels  168 us (98%)
    pallas_call x1, Pallas kernels, layer(): pl.pallas_call(layer_kernel, out_shape=[jax.ShapeDtypeStruct((PAIRS, LENG...  159 us
    pallas_call x1, Pallas kernels, finish(): pl.pallas_call(finish_kernel, grid=(steps,), out_shape=[jax.ShapeDtypeStr...  9.21 us

profile of v4, /device:TPU:0, one launch (start us, length us, event | category | flops | bytes accessed | tf_op | source)
XLA Modules:
  0.0 170.5 jit_solution(10944194423053835688)
XLA Ops:
  0.6 0.8 pad_add_fusion
  1.5 0.6 reshape.43.s_in
  2.1 159.0 %layer.1 = (bf16[2,280,768]{2,1,0:T(8,128)(2,1)}, bf16[2,280,768]{2,1,0:T(8,128)(2,1)}, bf16[1536,768]{1,0:T(8,128)(2,1)}, bf16[384,3072]{1,0:T(8,128)(2,1)}, bf...) custom-call(s32[2]{0:T(128)} %counts.1, bf16[2,280,768]{2,1,0:T(8,128)(2,1)} %tok.1, bf16[2,280,768]{2,1,0:T(8,128)(2,1)} %cot.1, ...), custom_call_target="tpu_custom_call" | custom-call | tf_op jit(solution)/shard_map/layer/pallas_call | solution.py:741
  161.1 9.2 %finish.1 = (f32[1536,768]{1,0:T(8,128)}, f32[384,3072]{1,0:T(8,128)}, f32[384,2304]{1,0:T(8,128)}, f32[384,768]{1,0:T(8,128)}, bf16[560,768]{1,0:T(8,128)(2,1)}...) custom-call(bf16[1536,768]{1,0:T(8,128)(2,1)} %get-tuple-element.34., ...), custom_call_target="tpu_custom_call" | custom-call | tf_op jit(solution)/shard_map/finish/pallas_call | solution.py:840

commit v5 on v4

--- a/solution.py
+++ b/solution.py
@@ -25,6 +25,7 @@
 SPLIT = 18
 PARTS = [(i, 0, None) for i in range(SPLIT)] + [(i, 128 * e, 128) for i in range(SPLIT, NCH) for e in range(2)]
 NP = len(PARTS)
+YFIRST = (1, 3, 5)
 GW = 5
 PIECES = (
     [(2, 4, 0, 96, FF // 2, FF // 8, 0, FF // 8)]
@@ -67,9 +68,9 @@
     ("F6", 13, 20), ("F7", 13, 21), ("F8", 13, 22), ("F9", 13, 22), ("F10", 13, 23), ("F11", 13, 24), ("G2",
     14, 25), ("G3", 15, 26), ("G4", 16, 26), ("H", 18, 27), ("I", 18, 29),
 )
-SLOTS = 2 * NP + 11
+SLOTS = 2 * NP + 17
 BY = [sum(p[0] < n for p in PARTS) for n in range(NCH + 1)]
-AHEAD, AHEAD_LAST, NARROW = 4, 4, 24
+AHEAD, AHEAD_LAST, NARROW = 6, 4, 24
 PLAN = plan()
 
 
@@ -127,7 +128,7 @@
     v0, v1, v2, v3,
     own, snd, ownd, sndd,
     cb, xb, yb, zb, stg, cbd, xbd, ybd, zbd, stgd, sacc, srecv,
-    gxs, gys, gcs, gzs, gsent, lsem, csent, rsent, csem, xsem, ysem, zsem, azsem, aysem, acsem, psem, ssem,
+    gxs, gys, gcs, gzs, gsent, lsem, csent, rsent, csem, xsem, ysem, zsem, zbsem, azsem, azasem, aysem, acsem, psem, ssem,
 ):
     f, core, y, z, peers = places()
     ins = (w0, w1, w2, w3)
@@ -135,6 +136,10 @@
     barrier = pltpu.get_barrier_semaphore()
     for name in peers:
         pl.semaphore_signal(barrier, inc=1, device_id=peers[name], device_id_type=MESH)
+    met = len(peers)
+    b0, b1 = lax.rem(z, 2), z // 2
+    dev = lax.axis_index("dp")
+    peers["p"] = (dev + 4 - 8 * b0, f)
 
     def send(src, dst, sent, arrived, name):
         return pltpu.make_async_remote_copy(
@@ -215,7 +220,7 @@
         local.append(pltpu.make_async_copy(ins[i], ws[i].at[pl.ds(pl.multiple_of(f * full, 16), full)], lsem.at[i]))
     local.append(pltpu.make_async_copy(s_in, smv.at[f], lsem.at[4]))
     local[4].start()
-    pl.semaphore_wait(barrier, len(peers))
+    pl.semaphore_wait(barrier, met)
     small_x = send(s_in, smv.at[f], ssem.at[0, 6], ssem.at[1, 6], "x")
     small_x.start()
     for g in range(GW):
@@ -246,21 +251,33 @@
         cc, xx, yy, zz, st = refs
         return ur, cc.at[j, :, :, at], xx.at[j, :, at], yy.at[j, :, at], zz.at[j, :, :, at], st.at[j, :, at]
 
+    def first_hop(n, e):
+        ur = bufs(n)[0]
+        if n in YFIRST:
+            g = 1 - f if e == 0 else f
+            return (g, ds((1 - y) * (ur // 2), ur // 2)), ds(g * (ur // 2), ur // 2), (g, ds(y * (ur // 2), ur // 2))
+        half = ds(((1 - y) if e == 0 else y) * (ur // 2), ur // 2)
+        return (1 - f, half), half, (f, half)
+
     def x_copy(h):
         n, e = h // 2, h % 2
-        ur, cc, xx, _, _, _ = bufs(n)
-        half = ds(((1 - y) if e == 0 else y) * (ur // 2), ur // 2)
-        return send(cc.at[1 - f, half], xx.at[half], rsent.at[0], xsem.at[h], "x")
+        _, cc, xx, _, _, _ = bufs(n)
+        there, here, _ = first_hop(n, e)
+        return send(cc.at[there], xx.at[here], rsent.at[0], xsem.at[h], "y" if n in YFIRST else "x")
 
     def y_copy(n):
-        ur, _, xx, yy, _, _ = bufs(n)
-        return send(xx.at[ds((1 - y) * (ur // 2), ur // 2)], yy, rsent.at[1], ysem.at[n], "y")
-
-    def z_copy(n, k):
+        _, _, xx, yy, _, _ = bufs(n)
+        return send(xx.at[first_hop(n, 0)[1]], yy, rsent.at[1], ysem.at[n], "x" if n in YFIRST else "y")
+
+    def za_copy(n, m):
         ur, _, _, yy, zz, _ = bufs(n)
-        return send(
-            yy.at[ds(lax.rem(z + k, NZ) * (ur // 8), ur // 8)], zz.at[k - 1], rsent.at[2], zsem.at[n], "z%d" % k
-        )
+        src = yy.at[ds((1 - b0) * (ur // 4) + m * (ur // 8), ur // 8, 16)]
+        return send(src, zz.at[m], rsent.at[2], zsem.at[n], "p")
+
+    def zb_copy(n):
+        ur, _, _, yy, zz, _ = bufs(n)
+        src = yy.at[ds(b0 * (ur // 4) + (1 - b1) * (ur // 8), ur // 8, 16)]
+        return send(src, zz.at[2], rsent.at[2], zbsem.at[n], "z2")
 
     def outpart(n, start, rows):
         i, c0, width = PARTS[n]
@@ -272,15 +289,20 @@
 
     def own_piece(n):
         ur, _, _, _, _, st = bufs(n)
-        return outpart(n, y * (ur // 2) + z * (ur // 8), ur // 8), st
+        return outpart(n, y * (ur // 2) + b0 * (ur // 4) + b1 * (ur // 8), ur // 8), st
 
     def p_copy(n):
         dst, src = own_piece(n)
         return pltpu.make_async_copy(src, dst, psem.at[n])
 
-    def az_copy(n, k):
+    def azb_copy(n):
         dst, src = own_piece(n)
-        return send(src, dst, rsent.at[3], azsem.at[n], "z%d" % k)
+        return send(src, dst, rsent.at[3], azsem.at[n], "z2")
+
+    def aza_copy(n):
+        ur = bufs(n)[0]
+        part = outpart(n, y * (ur // 2) + b0 * (ur // 4), ur // 4)
+        return send(part, part, rsent.at[3], azasem.at[n], "p")
 
     def ay_copy(n):
         ur = bufs(n)[0]
@@ -302,34 +324,43 @@
         x_copy(h).wait_recv()
         n = h // 2
         if h % 2 == 0:
-            ur, cc, xx, _, _, _ = bufs(n)
-            half = ds((1 - y) * (ur // 2), ur // 2)
-            xx[half] = (xx[half].astype(F32) + cc[f, half].astype(F32)).astype(BF16)
+            _, cc, xx, _, _, _ = bufs(n)
+            _, here, kept = first_hop(n, 0)
+            xx[here] = (xx[here].astype(F32) + cc[kept].astype(F32)).astype(BF16)
             y_copy(n).start()
 
     def s3(n):
         y_copy(n).wait_recv()
-        ur, cc, xx, yy, _, _ = bufs(n)
-        half = ds(y * (ur // 2), ur // 2)
-        yy[...] = (yy[...].astype(F32) + (xx[half].astype(F32) + cc[f, half].astype(F32))).astype(BF16)
-        for k in range(1, NZ):
-            z_copy(n, k).start()
+        _, cc, xx, yy, _, _ = bufs(n)
+        _, here, kept = first_hop(n, 1)
+        yy[...] = (yy[...].astype(F32) + (xx[here].astype(F32) + cc[kept].astype(F32))).astype(BF16)
+        for m in range(2):
+            za_copy(n, m).start()
+
+    def s3b(n):
+        ur, _, _, yy, zz, _ = bufs(n)
+        two = zz.at[pl.ds(0, 2)]
+        send(two, two, rsent.at[2], zsem.at[n], "p").wait_recv()
+        for m in range(2):
+            at = ds(b0 * (ur // 4) + m * (ur // 8), ur // 8, 16)
+            yy[at] = (yy[at].astype(F32) + zz[m].astype(F32)).astype(BF16)
+        zb_copy(n).start()
 
     def s4(n):
         ur, _, _, yy, zz, st = bufs(n)
-        send(zz, zz, rsent.at[2], zsem.at[n], "z1").wait_recv()
-        total = yy[ds(z * (ur // 8), ur // 8)].astype(F32)
-        for k in range(1, NZ):
-            total = total + zz[k - 1].astype(F32)
-        st[...] = total.astype(BF16)
+        zb_copy(n).wait_recv()
+        at = ds(b0 * (ur // 4) + b1 * (ur // 8), ur // 8, 16)
+        st[...] = (yy[at].astype(F32) + zz[2].astype(F32)).astype(BF16)
         p_copy(n).start()
-        for k in range(1, NZ):
-            az_copy(n, k).start()
+        azb_copy(n).start()
+
+    def s5a(n):
+        p_copy(n).wait()
+        azb_copy(n).wait_recv()
+        aza_copy(n).start()
 
     def s5(n):
-        p_copy(n).wait()
-        zz = bufs(n)[4]
-        send(zz, zz, rsent.at[3], azsem.at[n], "z1").wait_recv()
+        aza_copy(n).wait_recv()
         ay_copy(n).start()
 
     def s6(n):
@@ -339,7 +370,7 @@
     def slot(n):
         if n < 2 * NP:
             s2(n)
-        for lag, stage in ((3, s3), (6, s4), (9, s5), (12, s6)):
+        for lag, stage in ((3, s3), (6, s3b), (9, s4), (12, s5a), (15, s5), (18, s6)):
             if (n - lag) % 2 == 0 and 0 <= (n - lag) // 2 < NP:
                 stage((n - lag) // 2)
 
@@ -612,11 +643,7 @@
     s1(12, False)
     point("E")
 
-    def attend_back(i):
-        for when in range(12):
-            pl.when(i == when)(functools.partial(point, "F%d" % when))
-        p = i // 6
-        hp = lax.rem(i, 6)
+    def attend_back(p, hp):
         rows = ds(p * LPAD, LPAD)
         q = qkv[rows, ds(hp * 128, 128)]
         k = qkv[rows, ds(D + hp * 128, 128)]
@@ -640,7 +667,13 @@
             r = jnp.where(low, got3[0][part], got3[1][part]) * scale
             qkv[rows, ds(part * D + hp * 128, 128)] = r.astype(BF16)
 
-    loop(12, attend_back)
+    def heads_back(i):
+        for when in range(6):
+            pl.when(i == when)(lambda when=when: [point("F%d" % (2 * when + e)) for e in range(2)] and None)
+        for p in range(PAIRS):
+            attend_back(p, i)
+
+    loop(6, heads_back)
 
     def phase_g(t):
         @pl.when(t > 1)
@@ -800,6 +833,8 @@
             dma((NP,)),
             dma((NP,)),
             dma((NP,)),
+            dma((NP,)),
+            dma((NP,)),
             dma((1,)),
             dma((NP,)),
             dma((2, 7)),

time: 171 us -> 175 us (1.023)
  Pallas kernels: 168 us -> 172 us
    pallas_call x1, Pallas kernels: 159 us -> 163 us  [layer(): pl.pallas_call(layer_kernel, out_shape=[jax.ShapeDtypeStruct((PAIRS, LENG...]
where the time goes in v5:
time: 175 us; the launch traced here: 174 us
  Pallas kernels  172 us (98%)
    pallas_call x1, Pallas kernels, layer(): pl.pallas_call(layer_kernel, out_shape=[jax.ShapeDtypeStruct((PAIRS, LENG...  163 us
    pallas_call x1, Pallas kernels, finish(): pl.pallas_call(finish_kernel, grid=(steps,), out_shape=[jax.ShapeDtypeStr...  9.21 us

profile of v5, /device:TPU:0, one launch (start us, length us, event | category | flops | bytes accessed | tf_op | source)
XLA Modules:
  0.0 174.5 jit_solution(2285230188409739315)
XLA Ops:
  0.6 0.8 pad_add_fusion
  1.5 0.6 reshape.43.s_in
  2.1 163.0 %layer.1 = (bf16[2,280,768]{2,1,0:T(8,128)(2,1)}, bf16[2,280,768]{2,1,0:T(8,128)(2,1)}, bf16[1536,768]{1,0:T(8,128)(2,1)}, bf16[384,3072]{1,0:T(8,128)(2,1)}, bf...) custom-call(s32[2]{0:T(128)} %counts.1, bf16[2,280,768]{2,1,0:T(8,128)(2,1)} %tok.1, bf16[2,280,768]{2,1,0:T(8,128)(2,1)} %cot.1, ...), custom_call_target="tpu_custom_call" | custom-call | tf_op jit(solution)/shard_map/layer/pallas_call | solution.py:774
  165.1 9.2 %finish.1 = (f32[1536,768]{1,0:T(8,128)}, f32[384,3072]{1,0:T(8,128)}, f32[384,2304]{1,0:T(8,128)}, f32[384,768]{1,0:T(8,128)}, bf16[560,768]{1,0:T(8,128)(2,1)}...) custom-call(bf16[1536,768]{1,0:T(8,128)(2,1)} %get-tuple-element.34., ...), custom_call_target="tpu_custom_call" | custom-call | tf_op jit(solution)/shard_map/finish/pallas_call | solution.py:875
